TPU v7x, 32 devices: a whole 2x2x4 slice. The times are simulated.
32 devices in a mesh: grp: 2 (over x), dev: 16 (over z, y, core).
Axes of the slice: x: 2, y: 2, z: 4, core: 2. Of those that a mesh axis runs over, the one named last changes fastest.
Arguments:
- coords: float32 [16384, 64], P(('grp', 'dev')), may hold values from -6 to 6
- right_side: float32 [16384, 256], P(('grp', 'dev')), may hold values from -6 to 6
- leaf_perm: int32 [32, 512], P(('grp', 'dev')), may hold values from 0 to 511, each once within a row
- near_list: int32 [32, 4], P(('grp', 'dev')), may hold values from -1 to 31, as said below
- far_leaves: int32 [32, 4], P(('grp', 'dev')), may hold values from 0 to 31, as said below
- couplings: bfloat16 [32, 4, 128, 128], P(('grp', 'dev')), may hold values from -0.5 to 0.5
- transfer: bfloat16 [32, 128, 128], P(('grp', 'dev')), may hold values from -0.5 to 0.5
- leaf_basis: bfloat16 [16384, 128], P(('grp', 'dev')), may hold values from -0.25 to 0.25
- cluster_of: int32 [32], P(('grp', 'dev')), may hold values from 0 to 7, as said below
- far_clusters: int32 [8, 4], P('grp'), may hold values from 0 to 7, as said below
- cluster_couplings: bfloat16 [8, 4, 128, 128], P('grp'), may hold values from -0.25 to 0.25
- ridge_weight: float32 [], replicated, may hold values from 0.5 to 2
Outputs:
- solution: float32 [16384, 256], P(('grp', 'dev'))
- residual: float32 [16384, 256], P(('grp', 'dev'))
Inputs may be any that keep to these rules, and one draw needn't show every extreme that they name: `near_list`: each row lists leaves of the row's group whose position within the group differs from the row's leaf by 1 to 2, each at most once, in any slot order; -1 marks an empty slot. The number of listed leaves varies from leaf to leaf. `far_leaves`: each row names 4 different leaves of the row's group whose position within the group differs from the row's leaf by more than 2 and at most 8. `cluster_of`: leaves of group g belong to clusters g * 4 to g * 4 + 3, and every cluster holds exactly 4 leaves. `far_clusters`: each row names 4 different clusters, none of them in the row's own group.
All inputs are finite; a program needn't handle non-finite values.
Results may differ from a plain program's by a relative error of at most 0.0033.
Values may be sent and summed in bfloat16 or wider, within the bound.
A program may use at most 64 MiB of HBM per device.

v0:
```python
import functools

import jax
import jax.numpy as jnp
from jax import lax
from jax.experimental import pallas as pl
from jax.experimental.pallas import tpu as pltpu
from jax.sharding import PartitionSpec as P

MESH = pl.DeviceIdType.MESH
PARTS = 2

REACH = 2
FARREACH = 8
ITERS = 2


kernel_scale = 1.0 / 32.0
spectrum_gap = 0.5
spectrum_top = 8.0


def from_behind(shard, axis, by):
    devices = lax.axis_size(axis)
    pairs = [(i, i + by) for i in range(devices) if 0 <= i + by < devices]
    return lax.ppermute(shard, axis, pairs)


def kernel_block(left_points, right_points):
    inner_products = jnp.dot(
        left_points,
        right_points.T,
        precision=lax.Precision.HIGHEST,
        preferred_element_type=jnp.float32,
    )
    distance = (
        jnp.sum(left_points * left_points, axis=1)[:, None]
        + jnp.sum(right_points * right_points, axis=1)[None, :]
        - 2.0 * inner_products
    )
    return jnp.exp(-kernel_scale * distance).astype(jnp.bfloat16)


def body(
    coords,
    right_side,
    leaf_perm,
    near_list,
    far_leaves,
    couplings,
    transfer,
    leaf_basis,
    cluster_of,
    far_clusters,
    cluster_couplings,
    ridge_weight,
):
    dev_count = lax.axis_size("dev")
    group_index = lax.axis_index("grp")
    leaf_id = group_index * dev_count + lax.axis_index("dev")
    clusters_here = far_clusters.shape[0]
    local_cluster = cluster_of[0] - group_index * clusters_here
    ordering = leaf_perm[0]
    near_offsets = [offset for offset in range(-REACH, REACH + 1) if offset != 0]
    far_offsets = [offset for offset in range(-FARREACH, FARREACH + 1) if abs(offset) > REACH]
    neighbours = [from_behind(coords, "dev", -offset) for offset in near_offsets]
    near_flags = [
        jnp.any((near_list[0] == leaf_id + offset) & (near_list[0] >= 0)).astype(jnp.float32)
        for offset in near_offsets
    ]
    far_hits = jnp.stack(
        [far_leaves[0] == leaf_id + offset for offset in far_offsets], axis=1
    ).astype(jnp.bfloat16)
    own_block = kernel_block(coords, coords)
    near_blocks = [kernel_block(coords, neighbour_points) for neighbour_points in neighbours]
    cluster_slots = (jnp.arange(clusters_here) == local_cluster).astype(jnp.float32)

    def operate(direction):
        values = direction.astype(jnp.bfloat16)
        near_sum = jnp.dot(own_block, values, preferred_element_type=jnp.float32)
        for position in range(len(near_offsets)):
            remote = from_behind(values, "dev", -near_offsets[position])
            block_here = near_blocks[position]
            near_term = near_flags[position] * jnp.dot(
                block_here, remote, preferred_element_type=jnp.float32
            )
            near_sum = near_sum + near_term
        skeleton = lax.dot_general(
            leaf_basis,
            values[ordering],
            (((0,), (0,)), ((), ())),
            preferred_element_type=jnp.float32,
        ).astype(jnp.bfloat16)
        remote_skeletons = jnp.stack(
            [from_behind(skeleton, "dev", -offset) for offset in far_offsets]
        )
        chosen = jnp.einsum(
            "kj,jbo->kbo", far_hits, remote_skeletons, preferred_element_type=jnp.float32
        ).astype(jnp.bfloat16)
        level_one = jnp.einsum(
            "kab,kbo->ao", couplings[0], chosen, preferred_element_type=jnp.float32
        )
        uplift = lax.dot_general(
            transfer[0], skeleton, (((0,), (0,)), ((), ())), preferred_element_type=jnp.float32
        )
        contrib = cluster_slots[:, None, None] * uplift[None]
        column_sums = lax.psum_scatter(contrib, "dev", scatter_dimension=2, tiled=True).astype(
            jnp.bfloat16
        )
        every_column = lax.all_gather(column_sums, "grp", axis=0, tiled=True)
        picked = every_column[far_clusters]
        partial_coupled = jnp.einsum(
            "ckab,ckbo->cao", cluster_couplings, picked, preferred_element_type=jnp.float32
        ).astype(jnp.bfloat16)
        whole_columns = lax.all_gather(partial_coupled, "dev", axis=2, tiled=True)
        coupled = whole_columns[local_cluster]
        downward = jnp.dot(transfer[0], coupled, preferred_element_type=jnp.float32)
        tree_rows = jnp.dot(
            leaf_basis,
            (level_one + downward).astype(jnp.bfloat16),
            preferred_element_type=jnp.float32,
        )
        far_part = jnp.zeros_like(tree_rows).at[ordering].set(tree_rows)
        return ridge_weight * direction + (near_sum + far_part)

    bottom_edge = ridge_weight + spectrum_gap
    top_edge = ridge_weight + spectrum_top
    centre = (top_edge + bottom_edge) / 2.0
    spread = (top_edge - bottom_edge) / 2.0
    sigma_ratio = centre / spread
    contraction = 1.0 / sigma_ratio
    direction = right_side / centre
    solution = direction
    residual = right_side
    for rounds in range(ITERS):
        residual = residual - operate(direction)
        rho_next = 1.0 / (2.0 * sigma_ratio - contraction)
        direction = rho_next * contraction * direction + 2.0 * rho_next / spread * residual
        solution = solution + direction
        contraction = rho_next
    return (solution, residual)


def fused_kernel(
    n,
    coords_ref,
    right_ref,
    perm_ref,
    near_ref,
    far_ref,
    coup_ref,
    transfer_ref,
    basis_ref,
    cluster_ref,
    farclus_ref,
    cluscoup_ref,
    ridge_ref,
    sol_ref,
    res_ref,
    points,
    wide,
    blocks,
    skel,
    moved,
    spread_t,
    chosen,
    mine,
    theirs,
    coup_out,
    coup_in,
    basis_p,
    basis_t,
    acc,
    direction,
    near_send,
    near_recv,
    tree_send,
    tree_recv,
    mate_send,
    mate_recv,
    grp_send,
    grp_recv,
):
    f32, bf16 = jnp.float32, jnp.bfloat16
    group = lax.axis_index("grp")
    me = lax.axis_index("dev")
    other = 1 - group
    chips = n // 2
    chip = lax.div(me, 2)
    core = lax.rem(me, 2)
    row = lax.rem(chip, 2)
    mate = chip * 2 + (1 - core)
    across = me + 2 - 4 * row
    leaf, outs = right_ref.shape
    rank = transfer_ref.shape[1]
    clusters = cluscoup_ref.shape[0]
    has_z = ((row == 0) & (me >= 4)) | ((row == 1) & (me + 4 < n))
    sends_z = ((row == 0) & (me + 4 < n)) | ((row == 1) & (me >= 4))
    z_target = jnp.where(sends_z, me + 4 - 8 * row, me)

    barrier = pltpu.get_barrier_semaphore()
    for step in range(1, n):
        pl.semaphore_signal(
            barrier, inc=1, device_id={"dev": lax.rem(me + step, n)}, device_id_type=MESH
        )
    pl.semaphore_signal(barrier, inc=1, device_id={"grp": other}, device_id_type=MESH)

    def near_copy(buf, stage, source, slot, target, size, part):
        piece = size // PARTS
        return pltpu.make_async_remote_copy(
            src_ref=buf.at[pl.ds(source * size + part * piece, piece)],
            dst_ref=buf.at[pl.ds(slot * size + part * piece, piece)],
            send_sem=near_send.at[stage, slot, part],
            recv_sem=near_recv.at[stage, slot, part],
            device_id={"dev": target},
            device_id_type=MESH,
        )

    def near_start(buf, stage, size):
        for part in range(PARTS):
            near_copy(buf, stage, 0, 2, across, size, part).start()
        for part in range(PARTS):
            near_copy(buf, stage, 0, 1, mate, size, part).start()

        @pl.when(jnp.logical_not(has_z))
        def _():
            buf[pl.ds(3 * size, size), :] = jnp.zeros((size, buf.shape[1]), buf.dtype)

        @pl.when(jnp.logical_not(has_z) & (core == row))
        def _():
            buf[pl.ds(4 * size, size), :] = jnp.zeros((size, buf.shape[1]), buf.dtype)

    def near_relay(buf, stage, size):
        for part in range(PARTS):
            near_copy(buf, stage, 0, 2, across, size, part).wait_recv()

            @pl.when(sends_z)
            def _():
                near_copy(buf, stage, 2, 3, z_target, size, part).start()

            @pl.when(core == row)
            def _():
                near_copy(buf, stage, 2, 4, mate, size, part).start()

    def near_second(buf, stage, size):
        for part in range(PARTS):

            @pl.when(has_z)
            def _():
                near_copy(buf, stage, 2, 3, mate, size, part).wait_recv()

            @pl.when(has_z & (core != row))
            def _():
                near_copy(buf, stage, 3, 4, mate, size, part).start()

    def near_finish(buf, stage, size):
        for part in range(PARTS):
            near_copy(buf, stage, 0, 1, mate, size, part).wait_recv()

            @pl.when(has_z | (core != row))
            def _():
                near_copy(buf, stage, 0, 4, mate, size, part).wait_recv()

    def near_drain(buf, stage, size):
        for part in range(PARTS):
            near_copy(buf, stage, 0, 1, mate, size, part).wait_send()
            near_copy(buf, stage, 0, 2, across, size, part).wait_send()

            @pl.when(sends_z)
            def _():
                near_copy(buf, stage, 2, 3, z_target, size, part).wait_send()

            @pl.when(has_z | (core == row))
            def _():
                near_copy(buf, stage, 0, 4, mate, size, part).wait_send()

    def tree_block(buf, owner, size):
        return buf.at[pl.ds(pl.multiple_of(owner * size, 16), size)]

    def tree_copy(buf, stage, step, owner, target, size, send, recv):
        return pltpu.make_async_remote_copy(
            src_ref=tree_block(buf, owner, size),
            dst_ref=tree_block(buf, owner, size),
            send_sem=send.at[stage, step],
            recv_sem=recv.at[stage, step],
            device_id={"dev": target},
            device_id_type=MESH,
        )

    planes = chips // 2
    plane = lax.div(chip, 2)

    def along(step):
        return (lax.rem(plane + step % planes, planes) * 2 + row) * 2 + core

    def owner_of(step, side):
        flipped = row if step < planes else 1 - row
        return (lax.rem(plane - step % planes + planes, planes) * 2 + flipped) * 2 + side

    def tree_start(buf, stage, size):
        tree_copy(buf, stage, planes, me, across, size, tree_send, tree_recv).start()
        for step in range(1, planes):
            tree_copy(buf, stage, step, me, along(step), size, tree_send, tree_recv).start()
        tree_copy(buf, stage, 0, me, mate, size, mate_send, mate_recv).start()

    def tree_pass(buf, stage, step, size):
        owner = owner_of(step, core)
        tree_copy(buf, stage, step, owner, mate, size, mate_send, mate_recv).start()

    def tree_relay(buf, stage, size):
        for step in (planes, *range(1, planes), *range(planes + 1, chips)):
            owner = owner_of(step, core)
            tree_copy(buf, stage, step, owner, mate, size, tree_send, tree_recv).wait_recv()
            if step == planes:
                for later in range(planes + 1, chips):
                    tree_copy(
                        buf, stage, later, across, along(later), size, tree_send, tree_recv
                    ).start()
            tree_pass(buf, stage, step, size)

    def tree_finish(buf, stage, size):
        for step in range(chips):
            owner = owner_of(step, 1 - core)
            tree_copy(buf, stage, step, owner, mate, size, mate_send, mate_recv).wait_recv()

    def tree_drain(buf, stage, size):
        for step in range(chips):
            tree_copy(buf, stage, step, me, mate, size, mate_send, mate_recv).wait_send()
            if step > 0:
                tree_copy(buf, stage, step, me, mate, size, tree_send, tree_recv).wait_send()

    def grp_copy(source, target, stage):
        return pltpu.make_async_remote_copy(
            src_ref=source,
            dst_ref=target,
            send_sem=grp_send.at[stage],
            recv_sem=grp_recv.at[stage],
            device_id={"grp": other},
            device_id_type=MESH,
        )

    dim = coords_ref.shape[0]
    points[pl.ds(0, dim), :] = coords_ref[...]
    transfer_rows = transfer_ref[0]
    packed = rank + 16
    local_cluster = jnp.clip(cluster_ref[0] - group * clusters, 0, clusters - 1)
    lane_rows = lax.broadcasted_iota(jnp.int32, (16, rank), 0)
    tags = jnp.where(lane_rows == local_cluster, 1.0, 0.0).astype(bf16)
    own_rows = pl.multiple_of(me * packed, 16)
    moved[pl.ds(own_rows, rank), :] = transfer_rows.astype(f32).T.astype(bf16)
    moved[pl.ds(own_rows + rank, 16), :] = tags
    for place in range(clusters):
        total = jnp.zeros((rank, rank), f32)
        for k in range(farclus_ref.shape[1]):
            hit = (farclus_ref[local_cluster, k] == other * clusters + place).astype(f32)
            total = total + hit * cluscoup_ref[local_cluster, k].astype(f32)
        mine[:, place * rank : (place + 1) * rank] = total.astype(bf16)

    targets = lax.broadcasted_iota(jnp.int32, (leaf, leaf), 0)
    one_hot = jnp.where(targets == perm_ref[...], 1.0, 0.0).astype(bf16)
    placed = jnp.dot(one_hot, basis_ref[...], preferred_element_type=f32)
    basis_p[...] = placed.astype(bf16)
    basis_t[...] = placed.T.astype(bf16)
    ridge = ridge_ref[...]
    bottom_edge = ridge + spectrum_gap
    top_edge = ridge + spectrum_top
    centre = (top_edge + bottom_edge) / 2.0
    spread = (top_edge - bottom_edge) / 2.0
    sigma_ratio = centre / spread
    contraction = 1.0 / sigma_ratio
    start = right_ref[...] / centre
    direction[...] = start
    sol_ref[...] = start
    res_ref[...] = right_ref[...]

    def launch(rounds):
        values = direction[...].astype(bf16)
        wide[rounds, pl.ds(0, leaf), :] = values
        skeleton = jnp.dot(basis_t[...], values, preferred_element_type=f32).astype(bf16)
        skel[rounds, pl.ds(pl.multiple_of(me * rank, 16), rank), :] = skeleton
        tree_start(skel.at[rounds], rounds + 1, rank)
        near_start(wide.at[rounds], rounds + 1, leaf)

    pl.semaphore_wait(barrier, n)
    near_start(points, 0, dim)
    launch(0)
    tree_start(moved, 0, packed)
    grp_copy(mine, theirs, 0).start()

    for place in range(n):
        total = jnp.zeros((rank, rank), f32)
        for k in range(far_ref.shape[1]):
            hit = (far_ref[0, k] == group * n + place).astype(f32)
            total = total + hit * coup_ref[0, k].astype(f32)
        chosen[:, place * rank : (place + 1) * rank] = total.astype(bf16)

    left = coords_ref[...].T
    left_sq = jnp.sum(left * left, axis=1, keepdims=True)

    def fill_block(slot, source):
        right = points[pl.ds(slot * dim, dim), :]
        right_sq = jnp.sum(right * right, axis=0, keepdims=True)
        inner = jnp.dot(
            left, right, precision=lax.Precision.HIGHEST, preferred_element_type=f32
        )
        block = jnp.exp(-kernel_scale * (left_sq + right_sq - 2.0 * inner))
        if source is not None:
            wanted = group * n + source
            hit = jnp.float32(0.0)
            for k in range(near_ref.shape[1]):
                listed = (near_ref[0, k] == wanted) & (near_ref[0, k] >= 0)
                hit = hit + listed.astype(f32)
            block = hit * block
        blocks[:, slot * leaf : (slot + 1) * leaf] = block.astype(bf16)

    def spread_transfers():
        for place in range(n):
            part = moved[place * packed : place * packed + rank, :]
            for c in range(clusters):
                tag = moved[place * packed + rank : place * packed + packed, :][c : c + 1, :]
                spread_t[c * rank : (c + 1) * rank, place * rank : (place + 1) * rank] = (
                    part.astype(f32) * tag.astype(f32)
                ).astype(bf16)

    for rounds in range(ITERS):
        stage = rounds + 1
        if rounds > 0:
            launch(rounds)
        if rounds == 0:
            fill_block(0, None)
            near_relay(points, 0, dim)
            tree_relay(moved, 0, packed)
            near_second(points, 0, dim)
        acc[...] = ridge * direction[...] + jnp.dot(
            blocks[:, 0:leaf], wide[rounds, 0:leaf, :], preferred_element_type=f32
        )
        tree_relay(skel.at[rounds], stage, rank)
        near_relay(wide.at[rounds], stage, leaf)
        if rounds == 0:
            near_finish(points, 0, dim)
            fill_block(1, mate)
            fill_block(2, across)
            near_second(wide.at[rounds], stage, leaf)
            tree_finish(moved, 0, packed)
            spread_transfers()
            grp_copy(mine, theirs, 0).wait_recv()
        else:
            near_second(wide.at[rounds], stage, leaf)
        tree_finish(skel.at[rounds], stage, rank)
        sums = jnp.dot(spread_t[...], skel[rounds], preferred_element_type=f32).astype(bf16)
        coup_out[rounds] = jnp.dot(theirs[...], sums, preferred_element_type=f32).astype(bf16)
        grp_copy(coup_out.at[rounds], coup_in.at[rounds], stage).start()
        level_one = jnp.dot(chosen[...], skel[rounds], preferred_element_type=f32)
        if rounds == 0:
            fill_block(3, me - 2 + 4 * row)
            fill_block(4, me - 1 + 2 * core)
        near_finish(wide.at[rounds], stage, leaf)
        acc[...] += jnp.dot(
            blocks[:, leaf:], wide[rounds, leaf:, :], preferred_element_type=f32
        )
        grp_copy(coup_out.at[rounds], coup_in.at[rounds], stage).wait_recv()
        down = jnp.dot(transfer_rows, coup_in[rounds], preferred_element_type=f32)
        far_part = jnp.dot(
            basis_p[...], (level_one + down).astype(bf16), preferred_element_type=f32
        )
        residual = res_ref[...] - (acc[...] + far_part)
        res_ref[...] = residual
        rho_next = 1.0 / (2.0 * sigma_ratio - contraction)
        moved_on = rho_next * contraction * direction[...] + 2.0 * rho_next / spread * residual
        direction[...] = moved_on
        sol_ref[...] += moved_on
        contraction = rho_next

    near_drain(points, 0, dim)
    tree_drain(moved, 0, packed)
    grp_copy(mine, theirs, 0).wait_send()
    for rounds in range(ITERS):
        near_drain(wide.at[rounds], rounds + 1, leaf)
        tree_drain(skel.at[rounds], rounds + 1, rank)
        grp_copy(coup_out.at[rounds], coup_in.at[rounds], rounds + 1).wait_send()


def fused_body(
    coords,
    right_side,
    leaf_perm,
    near_list,
    far_leaves,
    couplings,
    transfer,
    leaf_basis,
    cluster_of,
    far_clusters,
    cluster_couplings,
    ridge_weight,
):
    n = lax.axis_size("dev")
    leaf, dim = coords.shape
    outs = right_side.shape[1]
    rank = transfer.shape[1]
    clusters = cluster_couplings.shape[0]
    bf16, f32 = jnp.bfloat16, jnp.float32
    vmem = pl.BlockSpec(memory_space=pltpu.VMEM)
    smem = pl.BlockSpec(memory_space=pltpu.SMEM)
    sem = pltpu.SemaphoreType.DMA
    stages = ITERS + 1
    out = jax.ShapeDtypeStruct((leaf, outs), f32)
    return pl.pallas_call(
        functools.partial(fused_kernel, n),
        out_shape=(out, out),
        in_specs=[vmem, vmem, vmem, smem, smem, vmem, vmem, vmem, smem, smem, vmem, vmem],
        out_specs=(vmem, vmem),
        scratch_shapes=[
            pltpu.VMEM((5 * dim, leaf), f32),
            pltpu.VMEM((ITERS, 5 * leaf, outs), bf16),
            pltpu.VMEM((leaf, 5 * leaf), bf16),
            pltpu.VMEM((ITERS, n * rank, outs), bf16),
            pltpu.VMEM((n * (rank + 16), rank), bf16),
            pltpu.VMEM((clusters * rank, n * rank), bf16),
            pltpu.VMEM((rank, n * rank), bf16),
            pltpu.VMEM((rank, clusters * rank), bf16),
            pltpu.VMEM((rank, clusters * rank), bf16),
            pltpu.VMEM((ITERS, rank, outs), bf16),
            pltpu.VMEM((ITERS, rank, outs), bf16),
            pltpu.VMEM((leaf, rank), bf16),
            pltpu.VMEM((rank, leaf), bf16),
            pltpu.VMEM((leaf, outs), f32),
            pltpu.VMEM((leaf, outs), f32),
            sem((stages, 5, PARTS)),
            sem((stages, 5, PARTS)),
            sem((stages, n // 2)),
            sem((stages, n // 2)),
            sem((stages, n // 2)),
            sem((stages, n // 2)),
            sem((stages,)),
            sem((stages,)),
        ],
        compiler_params=pltpu.CompilerParams(
            collective_id=0, has_side_effects=True, vmem_limit_bytes=48 << 20
        ),
        name="fused_solve",
    )(
        coords.T,
        right_side,
        leaf_perm,
        near_list,
        far_leaves,
        couplings,
        transfer,
        leaf_basis,
        cluster_of,
        far_clusters,
        cluster_couplings,
        ridge_weight.reshape(1, 1),
    )


def solution(mesh):
    fits = mesh.shape["grp"] == 2 and mesh.shape["dev"] % 4 == 0
    placed = (
        P(("grp", "dev"), None),
        P(("grp", "dev"), None),
        P(("grp", "dev"), None),
        P(("grp", "dev"), None),
        P(("grp", "dev"), None),
        P(("grp", "dev"), None, None, None),
        P(("grp", "dev"), None, None),
        P(("grp", "dev"), None),
        P(("grp", "dev")),
        P("grp", None),
        P("grp", None, None, None),
        P(),
    )
    return jax.shard_map(
        fused_body if fits else body,
        mesh=mesh,
        in_specs=placed,
        out_specs=(P(("grp", "dev"), None), P(("grp", "dev"), None)),
        check_vma=False,
    )
```

profile of v0, /device:TPU:4, one launch (start us, length us, event | category | flops | bytes accessed | tf_op | source)
XLA Modules:
  0.0 74.4 jit_solution(57877308439913354)
XLA Ops:
  1.3 0.0 copy-start.7
  1.3 0.0 copy-start.6
  2.0 0.0 copy-start.8
  2.0 0.0 copy-start.9
  2.0 0.0 copy-done.7
  2.0 0.0 copy-done.6
  2.0 0.6 copy-done.8
  2.6 0.0 copy-done.9
  2.6 0.0 copy-start
  2.6 1.0 %copy-done = f32[512,256]{1,0:T(8,128)S(1)} copy-done((f32[512,256]{1,0:T(8,128)S(1)}, f32[512,256]{1,0:T(8,128)}, u32[]{:S(2)}) %copy-start) | copy-done | bytes 524312
  3.7 0.0 copy-start.1
  3.7 1.0 %copy-done.1 = bf16[4,4,128,128]{3,2,1,0:T(8,128)(2,1)S(1)} copy-done((bf16[4,4,128,128]{3,2,1,0:T(8,128)(2,1)S(1)}, bf16[4,4,128,128]{3,2,1,0:T(8,128)(2,1)}, u32[]{:S(2)}) %copy-start.1) | copy-done | bytes 524312
  4.7 0.0 copy-start.2
  4.7 0.9 %copy-done.2 = f32[512,64]{0,1:T(8,128)S(1)} copy-done((f32[512,64]{0,1:T(8,128)S(1)}, f32[512,64]{0,1:T(8,128)}, u32[]{:S(2)}) %copy-start.2) | copy-done | bytes 131096
  5.6 0.0 copy-start.3
  5.6 0.9 %copy-done.3 = bf16[1,4,128,128]{3,2,1,0:T(8,128)(2,1)S(1)} copy-done((bf16[1,4,128,128]{3,2,1,0:T(8,128)(2,1)S(1)}, bf16[1,4,128,128]{3,2,1,0:T(8,128)(2,1)}, u32[]{:S(2)}) %copy-start.3) | copy-done | bytes 131096
  6.5 0.0 copy-start.4
  6.5 0.9 %copy-done.4 = bf16[512,128]{1,0:T(8,128)(2,1)S(1)} copy-done((bf16[512,128]{1,0:T(8,128)(2,1)S(1)}, bf16[512,128]{1,0:T(8,128)(2,1)}, u32[]{:S(2)}) %copy-start.4) | copy-done | bytes 131096
  7.4 0.0 copy-start.5
  7.4 0.8 %copy-done.5 = bf16[1,128,128]{2,1,0:T(8,128)(2,1)S(1)} copy-done((bf16[1,128,128]{2,1,0:T(8,128)(2,1)S(1)}, bf16[1,128,128]{2,1,0:T(8,128)(2,1)}, u32[]{:S(2)}) %copy-start.5) | copy-done | bytes 32792
  8.2 64.6 %fused_solve.1 = (f32[512,256]{1,0:T(8,128)S(1)}, f32[512,256]{1,0:T(8,128)S(1)}) custom-call(f32[64,512]{1,0:T(8,128)S(1)} %bitcast.3, f32[512,256]{1,0:T(8,128)S(1)} %copy-done, s32[1,512]{1,0:T(1,128)S(1)} %copy-done.6, s32[1,4]{1,0:T(1,128)S(1)} %copy-done.8, s32[1,4]{1,0:T(1,128)S(1)} %copy-done.9, bf16[1,4,128,128]{3,2,1,0:T(8,128)(2,1)S(1)} %copy-done.3, ...), custom_call_target="tpu_custom_call" | custom-call | tf_op jit(solution)/shard_map/fused_solve/pallas_call | solution.py:508
  72.8 0.8 %copy.18 = f32[512,256]{1,0:T(8,128)} copy(f32[512,256]{1,0:T(8,128)S(1)} %get-tuple-element.4) | data formatting | bytes 1048576
  73.6 0.8 %copy.19 = f32[512,256]{1,0:T(8,128)} copy(f32[512,256]{1,0:T(8,128)S(1)} %get-tuple-element.5) | data formatting | bytes 1048576
Async XLA Ops:
  1.3 0.7 copy-start.7
  1.3 0.7 copy-start.6
  2.0 0.7 copy-start.8
  2.0 0.7 copy-start.9
  2.6 1.0 %copy-start = (f32[512,256]{1,0:T(8,128)S(1)}, f32[512,256]{1,0:T(8,128)}, u32[]{:S(2)}) copy-start(f32[512,256]{1,0:T(8,128)} %right_ref.1) | copy-start | bytes 1572868
  3.7 1.0 %copy-start.1 = (bf16[4,4,128,128]{3,2,1,0:T(8,128)(2,1)S(1)}, bf16[4,4,128,128]{3,2,1,0:T(8,128)(2,1)}, u32[]{:S(2)}) copy-start(bf16[4,4,128,128]{3,2,1,0:T(8,128)(2,1)} %cluscoup_ref.1) | copy-start | bytes 1572868
  4.7 0.9 %copy-start.2 = (f32[512,64]{0,1:T(8,128)S(1)}, f32[512,64]{0,1:T(8,128)}, u32[]{:S(2)}) copy-start(f32[512,64]{0,1:T(8,128)} %param.12) | copy-start | bytes 393220
  5.6 0.9 %copy-start.3 = (bf16[1,4,128,128]{3,2,1,0:T(8,128)(2,1)S(1)}, bf16[1,4,128,128]{3,2,1,0:T(8,128)(2,1)}, u32[]{:S(2)}) copy-start(bf16[1,4,128,128]{3,2,1,0:T(8,128)(2,1)} %coup_ref.1) | copy-start | bytes 393220
  6.5 0.9 %copy-start.4 = (bf16[512,128]{1,0:T(8,128)(2,1)S(1)}, bf16[512,128]{1,0:T(8,128)(2,1)}, u32[]{:S(2)}) copy-start(bf16[512,128]{1,0:T(8,128)(2,1)} %basis_ref.1) | copy-start | bytes 393220
  7.4 0.8 %copy-start.5 = (bf16[1,128,128]{2,1,0:T(8,128)(2,1)S(1)}, bf16[1,128,128]{2,1,0:T(8,128)(2,1)}, u32[]{:S(2)}) copy-start(bf16[1,128,128]{2,1,0:T(8,128)(2,1)} %transfer_ref.1) | copy-start | bytes 98308
where the time goes:
time: 74.8 us; the launch traced here: 74.4 us
  Pallas kernels  64.6 us (86%)
  local copies, waits for them, and re-layouts  7.78 us (10%)
  between operations  2.01 us (3%)
    pallas_call x1, Pallas kernels, fused_body(): pl.pallas_call(functools.partial(fused_kernel, n), out_shape=(out, out),...  64.6 us
    unnamed x22, local copies, waits for them, and re-layouts  7.78 us

commit v1 on v0

--- a/solution.py
+++ b/solution.py
@@ -9,6 +9,7 @@
 
 MESH = pl.DeviceIdType.MESH
 PARTS = 2
+EARLY = 1
 
 REACH = 2
 FARREACH = 8
@@ -143,67 +144,98 @@
 
 def fused_kernel(
     n,
-    coords_ref,
-    right_ref,
-    perm_ref,
-    near_ref,
-    far_ref,
-    coup_ref,
-    transfer_ref,
-    basis_ref,
+    coords_hbm,
+    right_hbm,
+    perm_hbm,
+    near_hbm,
+    far_hbm,
+    coup_hbm,
+    transfer_hbm,
+    basis_hbm,
     cluster_ref,
-    farclus_ref,
-    cluscoup_ref,
-    ridge_ref,
+    farclus_hbm,
+    cluscoup_hbm,
+    ridge_hbm,
     sol_ref,
     res_ref,
     points,
     wide,
     blocks,
     skel,
-    moved,
-    spread_t,
-    chosen,
-    mine,
-    theirs,
-    coup_out,
-    coup_in,
+    up_out,
+    up_in,
+    tag_in,
+    sums_t,
+    pair_map,
+    partners,
+    c_out,
+    c_in,
     basis_p,
     basis_t,
     acc,
     direction,
+    perm_ref,
+    basis_ref,
+    transfer_ref,
+    coup_ref,
+    cluscoup_ref,
+    ridge_ref,
+    near_ref,
+    far_ref,
+    farclus_ref,
+    load_sem,
     near_send,
     near_recv,
     tree_send,
     tree_recv,
-    mate_send,
-    mate_recv,
-    grp_send,
-    grp_recv,
+    wide_send,
+    wide_recv,
 ):
     f32, bf16 = jnp.float32, jnp.bfloat16
     group = lax.axis_index("grp")
     me = lax.axis_index("dev")
     other = 1 - group
-    chips = n // 2
     chip = lax.div(me, 2)
     core = lax.rem(me, 2)
     row = lax.rem(chip, 2)
     mate = chip * 2 + (1 - core)
     across = me + 2 - 4 * row
-    leaf, outs = right_ref.shape
-    rank = transfer_ref.shape[1]
-    clusters = cluscoup_ref.shape[0]
+    across_mate = mate + 2 - 4 * row
+    leaf, outs = right_hbm.shape
+    dim = coords_hbm.shape[0]
+    rank = transfer_hbm.shape[1]
+    clusters = cluscoup_hbm.shape[0]
+    width = outs // n
+    tag_rows = 16
     has_z = ((row == 0) & (me >= 4)) | ((row == 1) & (me + 4 < n))
     sends_z = ((row == 0) & (me + 4 < n)) | ((row == 1) & (me >= 4))
     z_target = jnp.where(sends_z, me + 4 - 8 * row, me)
 
     barrier = pltpu.get_barrier_semaphore()
-    for step in range(1, n):
+    for step in range(n):
+        place = lax.rem(me + step, n)
         pl.semaphore_signal(
-            barrier, inc=1, device_id={"dev": lax.rem(me + step, n)}, device_id_type=MESH
-        )
-    pl.semaphore_signal(barrier, inc=1, device_id={"grp": other}, device_id_type=MESH)
+            barrier, inc=1, device_id={"grp": other, "dev": place}, device_id_type=MESH
+        )
+        if step > 0:
+            pl.semaphore_signal(barrier, inc=1, device_id={"dev": place}, device_id_type=MESH)
+
+    loads = {}
+    for name, source, target in (
+        ("perm", perm_hbm, perm_ref),
+        ("basis", basis_hbm, basis_ref),
+        ("ridge", ridge_hbm, ridge_ref),
+        ("right", right_hbm, res_ref),
+        ("transfer", transfer_hbm, transfer_ref),
+        ("coords", coords_hbm, points.at[pl.ds(0, dim)]),
+        ("near", near_hbm, near_ref),
+        ("far", far_hbm, far_ref),
+        ("farclus", farclus_hbm, farclus_ref),
+        ("cluscoup", cluscoup_hbm, cluscoup_ref),
+        ("coup", coup_hbm, coup_ref),
+    ):
+        loads[name] = pltpu.make_async_copy(source, target, load_sem.at[len(loads)])
+        loads[name].start()
 
     def near_copy(buf, stage, source, slot, target, size, part):
         piece = size // PARTS
@@ -230,8 +262,8 @@
         def _():
             buf[pl.ds(4 * size, size), :] = jnp.zeros((size, buf.shape[1]), buf.dtype)
 
-    def near_relay(buf, stage, size):
-        for part in range(PARTS):
+    def near_relay(buf, stage, size, parts):
+        for part in parts:
             near_copy(buf, stage, 0, 2, across, size, part).wait_recv()
 
             @pl.when(sends_z)
@@ -253,9 +285,12 @@
             def _():
                 near_copy(buf, stage, 3, 4, mate, size, part).start()
 
+    def near_first(buf, stage, size):
+        for part in range(PARTS):
+            near_copy(buf, stage, 0, 1, mate, size, part).wait_recv()
+
     def near_finish(buf, stage, size):
         for part in range(PARTS):
-            near_copy(buf, stage, 0, 1, mate, size, part).wait_recv()
 
             @pl.when(has_z | (core != row))
             def _():
@@ -274,93 +309,155 @@
             def _():
                 near_copy(buf, stage, 0, 4, mate, size, part).wait_send()
 
-    def tree_block(buf, owner, size):
-        return buf.at[pl.ds(pl.multiple_of(owner * size, 16), size)]
-
-    def tree_copy(buf, stage, step, owner, target, size, send, recv):
+    heading = 1 - 2 * row
+
+    def inside(owner):
+        return (owner >= 0) & (owner < n)
+
+    def tree_copy(rounds, step, owner, target):
+        owner = jnp.clip(owner, 0, n - 1)
+        place = pl.ds(pl.multiple_of(owner * rank, 16), rank)
         return pltpu.make_async_remote_copy(
-            src_ref=tree_block(buf, owner, size),
-            dst_ref=tree_block(buf, owner, size),
-            send_sem=send.at[stage, step],
-            recv_sem=recv.at[stage, step],
-            device_id={"dev": target},
+            src_ref=skel.at[rounds, place],
+            dst_ref=skel.at[rounds, place],
+            send_sem=tree_send.at[rounds, step],
+            recv_sem=tree_recv.at[rounds, owner],
+            device_id={"dev": jnp.clip(target, 0, n - 1)},
             device_id_type=MESH,
         )
 
-    planes = chips // 2
-    plane = lax.div(chip, 2)
-
-    def along(step):
-        return (lax.rem(plane + step % planes, planes) * 2 + row) * 2 + core
-
-    def owner_of(step, side):
-        flipped = row if step < planes else 1 - row
-        return (lax.rem(plane - step % planes + planes, planes) * 2 + flipped) * 2 + side
-
-    def tree_start(buf, stage, size):
-        tree_copy(buf, stage, planes, me, across, size, tree_send, tree_recv).start()
-        for step in range(1, planes):
-            tree_copy(buf, stage, step, me, along(step), size, tree_send, tree_recv).start()
-        tree_copy(buf, stage, 0, me, mate, size, mate_send, mate_recv).start()
-
-    def tree_pass(buf, stage, step, size):
-        owner = owner_of(step, core)
-        tree_copy(buf, stage, step, owner, mate, size, mate_send, mate_recv).start()
-
-    def tree_relay(buf, stage, size):
-        for step in (planes, *range(1, planes), *range(planes + 1, chips)):
-            owner = owner_of(step, core)
-            tree_copy(buf, stage, step, owner, mate, size, tree_send, tree_recv).wait_recv()
-            if step == planes:
-                for later in range(planes + 1, chips):
-                    tree_copy(
-                        buf, stage, later, across, along(later), size, tree_send, tree_recv
-                    ).start()
-            tree_pass(buf, stage, step, size)
-
-    def tree_finish(buf, stage, size):
-        for step in range(chips):
-            owner = owner_of(step, 1 - core)
-            tree_copy(buf, stage, step, owner, mate, size, mate_send, mate_recv).wait_recv()
-
-    def tree_drain(buf, stage, size):
-        for step in range(chips):
-            tree_copy(buf, stage, step, me, mate, size, mate_send, mate_recv).wait_send()
-            if step > 0:
-                tree_copy(buf, stage, step, me, mate, size, tree_send, tree_recv).wait_send()
-
-    def grp_copy(source, target, stage):
+    along = (1, -1, 2, -2)
+    own_sends = [(inside(me + 4 * dz), me, me + 4 * dz) for dz in along]
+    own_sends.append((core == row, me, across_mate))
+    lane_waits, lane_sends = [], []
+    for dz in along:
+        owner = me - 4 * dz
+        here = inside(owner)
+        lane_waits.append((here, owner))
+        passes = here
+        if dz == 2:
+            passes = here & (core == 1)
+        if dz == -2:
+            passes = here & (core == 0)
+        full = (heading == dz) | (heading * -2 == dz)
+        part = (heading == -dz) & (core == 1 - row)
+        lane_sends.append(
+            [(passes, owner, mate), (here & (full | part), owner, jnp.where(part, across_mate, across))]
+        )
+    side_waits = [
+        (inside(across + 4 * heading), across + 4 * heading),
+        (inside(across - 8 * heading), across - 8 * heading),
+    ]
+    side_sends = [(here, owner, mate) for here, owner in side_waits]
+    last_waits = [
+        (core == row, across_mate),
+        ((core == 1 - row) & inside(across_mate - 4 * heading), across_mate - 4 * heading),
+        (inside(mate - 4), mate - 4),
+        (inside(mate + 4), mate + 4),
+        ((core == 0) & inside(mate - 8), mate - 8),
+        ((core == 1) & inside(mate + 8), mate + 8),
+        (inside(across_mate + 4 * heading), across_mate + 4 * heading),
+        (inside(across_mate - 8 * heading), across_mate - 8 * heading),
+    ]
+    every_send = own_sends + [pair for pairs in lane_sends for pair in pairs] + side_sends
+
+    def tree_go(rounds, first, sends):
+        for step, (when, owner, target) in enumerate(sends):
+
+            @pl.when(when)
+            def _():
+                tree_copy(rounds, first + step, owner, target).start()
+
+    def tree_wait(rounds, waits):
+        for when, owner in waits:
+
+            @pl.when(when)
+            def _():
+                tree_copy(rounds, 0, owner, mate).wait_recv()
+
+    def tree_lanes(rounds, chosen):
+        for lane in chosen:
+            tree_wait(rounds, lane_waits[lane : lane + 1])
+            tree_go(rounds, len(own_sends) + 2 * lane, lane_sends[lane])
+
+    def tree_sides(rounds):
+        for side in range(2):
+            tree_wait(rounds, side_waits[side : side + 1])
+            tree_go(rounds, len(every_send) - 2 + side, side_sends[side : side + 1])
+
+    def tree_drain(rounds):
+        for step, (when, owner, target) in enumerate(every_send):
+
+            @pl.when(when)
+            def _():
+                tree_copy(rounds, step, owner, target).wait_send()
+
+    def wide_copy(source, target, sem, device):
         return pltpu.make_async_remote_copy(
             src_ref=source,
             dst_ref=target,
-            send_sem=grp_send.at[stage],
-            recv_sem=grp_recv.at[stage],
-            device_id={"grp": other},
+            send_sem=wide_send.at[sem],
+            recv_sem=wide_recv.at[sem],
+            device_id=device,
             device_id_type=MESH,
         )
 
-    dim = coords_ref.shape[0]
-    points[pl.ds(0, dim), :] = coords_ref[...]
-    transfer_rows = transfer_ref[0]
-    packed = rank + 16
-    local_cluster = jnp.clip(cluster_ref[0] - group * clusters, 0, clusters - 1)
-    lane_rows = lax.broadcasted_iota(jnp.int32, (16, rank), 0)
+    def up_rows(rounds):
+        return width + tag_rows if rounds == 0 else width
+
+    def up_start(rounds):
+        for step in range(n):
+            place = lax.rem(me + n // 2 + step, n)
+            rows = pl.ds(0, up_rows(rounds))
+            wide_copy(
+                up_out.at[rounds, place, rows],
+                up_in.at[rounds, me, rows],
+                rounds,
+                {"grp": other, "dev": place},
+            ).start()
+
+    def up_all(rounds):
+        whole = up_in.at[rounds, pl.ds(0, n), pl.ds(0, up_rows(rounds))]
+        return wide_copy(whole, whole, rounds, {"grp": other})
+
+    def tag_start():
+        for step in range(1, n):
+            place = lax.rem(me + step, n)
+            wide_copy(tag_in.at[me], tag_in.at[me], ITERS, {"dev": place}).start()
+
+    def tag_all():
+        whole = tag_in.at[pl.ds(0, n - 1)]
+        return wide_copy(whole, whole, ITERS, {"dev": mate})
+
+    def down_start(rounds):
+        for step in range(1, n):
+            place = lax.rem(me + step, n)
+            wide_copy(
+                c_out.at[rounds, place],
+                c_in.at[rounds, me],
+                ITERS + 1 + rounds,
+                {"dev": place},
+            ).start()
+
+    def down_all(rounds):
+        whole = c_in.at[rounds, pl.ds(0, n - 1)]
+        return wide_copy(whole, whole, ITERS + 1 + rounds, {"dev": mate})
+
+    local_cluster = cluster_ref[0] - group * clusters
+    lane_rows = lax.broadcasted_iota(jnp.int32, (tag_rows, rank), 0)
     tags = jnp.where(lane_rows == local_cluster, 1.0, 0.0).astype(bf16)
-    own_rows = pl.multiple_of(me * packed, 16)
-    moved[pl.ds(own_rows, rank), :] = transfer_rows.astype(f32).T.astype(bf16)
-    moved[pl.ds(own_rows + rank, 16), :] = tags
-    for place in range(clusters):
-        total = jnp.zeros((rank, rank), f32)
-        for k in range(farclus_ref.shape[1]):
-            hit = (farclus_ref[local_cluster, k] == other * clusters + place).astype(f32)
-            total = total + hit * cluscoup_ref[local_cluster, k].astype(f32)
-        mine[:, place * rank : (place + 1) * rank] = total.astype(bf16)
-
+    tag_in[me] = tags
+    for place in range(n):
+        up_out[0, place, width:, :] = tags
+
+    loads["perm"].wait()
     targets = lax.broadcasted_iota(jnp.int32, (leaf, leaf), 0)
     one_hot = jnp.where(targets == perm_ref[...], 1.0, 0.0).astype(bf16)
+    loads["basis"].wait()
     placed = jnp.dot(one_hot, basis_ref[...], preferred_element_type=f32)
     basis_p[...] = placed.astype(bf16)
     basis_t[...] = placed.T.astype(bf16)
+    loads["ridge"].wait()
     ridge = ridge_ref[...]
     bottom_edge = ridge + spectrum_gap
     top_edge = ridge + spectrum_top
@@ -368,33 +465,84 @@
     spread = (top_edge - bottom_edge) / 2.0
     sigma_ratio = centre / spread
     contraction = 1.0 / sigma_ratio
-    start = right_ref[...] / centre
+    loads["right"].wait()
+    start = res_ref[...] / centre
     direction[...] = start
     sol_ref[...] = start
-    res_ref[...] = right_ref[...]
-
-    def launch(rounds):
+    loads["transfer"].wait()
+    transfer_rows = transfer_ref[0]
+
+    def prepare(rounds):
         values = direction[...].astype(bf16)
         wide[rounds, pl.ds(0, leaf), :] = values
-        skeleton = jnp.dot(basis_t[...], values, preferred_element_type=f32).astype(bf16)
-        skel[rounds, pl.ds(pl.multiple_of(me * rank, 16), rank), :] = skeleton
-        tree_start(skel.at[rounds], rounds + 1, rank)
+        skeleton = jnp.dot(basis_t[...], values, preferred_element_type=f32)
+        skel[rounds, pl.ds(pl.multiple_of(me * rank, 16), rank), :] = skeleton.astype(bf16)
+        uplift = jnp.dot(
+            skeleton.T.astype(bf16), transfer_rows, preferred_element_type=f32
+        ).astype(bf16)
+        for place in range(n):
+            up_out[rounds, place, 0:width, :] = uplift[place * width : (place + 1) * width, :]
+
+    def send(rounds):
+        up_start(rounds)
         near_start(wide.at[rounds], rounds + 1, leaf)
-
-    pl.semaphore_wait(barrier, n)
-    near_start(points, 0, dim)
-    launch(0)
-    tree_start(moved, 0, packed)
-    grp_copy(mine, theirs, 0).start()
-
-    for place in range(n):
-        total = jnp.zeros((rank, rank), f32)
-        for k in range(far_ref.shape[1]):
-            hit = (far_ref[0, k] == group * n + place).astype(f32)
-            total = total + hit * coup_ref[0, k].astype(f32)
-        chosen[:, place * rank : (place + 1) * rank] = total.astype(bf16)
-
-    left = coords_ref[...].T
+        tree_go(rounds, 0, own_sends)
+
+    def map_clusters():
+        for c in range(clusters):
+            for place in range(clusters):
+                total = jnp.zeros((rank, rank), f32)
+                for k in range(farclus_ref.shape[1]):
+                    hit = (farclus_ref[c, k] == other * clusters + place).astype(f32)
+                    total = total + hit * cluscoup_ref[c, k].astype(f32)
+                pair_map[place * rank : (place + 1) * rank, c * rank : (c + 1) * rank] = (
+                    total.T.astype(bf16)
+                )
+
+    def map_partners():
+        for place in range(n):
+            total = jnp.zeros((rank, rank), f32)
+            for k in range(far_ref.shape[1]):
+                hit = (far_ref[0, k] == group * n + place).astype(f32)
+                total = total + hit * coup_ref[0, k].astype(f32)
+            partners[:, place * rank : (place + 1) * rank] = total.astype(bf16)
+
+            @pl.when((jnp.abs(me - place) <= REACH) | (jnp.abs(me - place) > FARREACH))
+            def _():
+                for rounds in range(ITERS):
+                    if rounds > 0 :
+                        skel[rounds, place * rank : (place + 1) * rank, :] = jnp.zeros(
+                            (rank, outs), bf16
+                        )
+
+                @pl.when(me != place)
+                def _():
+                    skel[0, place * rank : (place + 1) * rank, :] = jnp.zeros((rank, outs), bf16)
+
+    def couple(rounds):
+        up_all(rounds).wait_recv()
+        totals = [jnp.zeros((width, rank), f32) for _ in range(clusters)]
+        for place in range(n):
+            part = up_in[rounds, place, 0:width, :].astype(f32)
+            tag = up_in[0, place, width:, :].astype(f32)
+            totals = [totals[c] + tag[c : c + 1, :] * part for c in range(clusters)]
+        for c in range(clusters):
+            sums_t[:, c * rank : (c + 1) * rank] = totals[c].astype(bf16)
+        coupled = jnp.dot(sums_t[...], pair_map[...], preferred_element_type=f32)
+        coupled = coupled.astype(bf16).astype(f32)
+        if rounds == 0:
+            tag_all().wait_recv()
+        for place in range(n):
+            tag = tag_in[place].astype(f32)
+            pick = jnp.zeros((width, rank), f32)
+            for c in range(clusters):
+                pick = pick + tag[c : c + 1, :] * coupled[:, c * rank : (c + 1) * rank]
+            c_out[rounds, place] = pick.astype(bf16)
+        c_in[rounds, me] = c_out[rounds, me]
+        down_start(rounds)
+
+    loads["coords"].wait()
+    left = points[pl.ds(0, dim), :].T
     left_sq = jnp.sum(left * left, axis=1, keepdims=True)
 
     def fill_block(slot, source):
@@ -413,53 +561,63 @@
             block = hit * block
         blocks[:, slot * leaf : (slot + 1) * leaf] = block.astype(bf16)
 
-    def spread_transfers():
-        for place in range(n):
-            part = moved[place * packed : place * packed + rank, :]
-            for c in range(clusters):
-                tag = moved[place * packed + rank : place * packed + packed, :][c : c + 1, :]
-                spread_t[c * rank : (c + 1) * rank, place * rank : (place + 1) * rank] = (
-                    part.astype(f32) * tag.astype(f32)
-                ).astype(bf16)
-
+    def near_dot(rounds, first, last):
+        return jnp.dot(
+            blocks[:, first * leaf : last * leaf],
+            wide[rounds, first * leaf : last * leaf, :],
+            preferred_element_type=f32,
+        )
+
+    prepare(0)
+    pl.semaphore_wait(barrier, 2 * n - 1)
+    up_start(0)
+    tag_start()
+    near_start(points, 0, dim)
+    near_start(wide.at[0], 1, leaf)
+    tree_go(0, 0, own_sends)
+    every = range(PARTS)
     for rounds in range(ITERS):
         stage = rounds + 1
         if rounds > 0:
-            launch(rounds)
+            prepare(rounds)
+            send(rounds)
+        else:
+            fill_block(0, None)
+            loads["farclus"].wait()
+            loads["cluscoup"].wait()
+            map_clusters()
+            loads["far"].wait()
+            loads["coup"].wait()
+            map_partners()
+            near_relay(points, 0, dim, every)
+        acc[...] = ridge * direction[...] + near_dot(rounds, 0, 1)
+        near_relay(wide.at[rounds], stage, leaf, every[:EARLY])
+        couple(rounds)
+        near_relay(wide.at[rounds], stage, leaf, every[EARLY:])
+        tree_lanes(rounds, range(4))
+        near_first(wide.at[rounds], stage, leaf)
         if rounds == 0:
-            fill_block(0, None)
-            near_relay(points, 0, dim)
-            tree_relay(moved, 0, packed)
-            near_second(points, 0, dim)
-        acc[...] = ridge * direction[...] + jnp.dot(
-            blocks[:, 0:leaf], wide[rounds, 0:leaf, :], preferred_element_type=f32
-        )
-        tree_relay(skel.at[rounds], stage, rank)
-        near_relay(wide.at[rounds], stage, leaf)
-        if rounds == 0:
-            near_finish(points, 0, dim)
+            loads["near"].wait()
+            near_first(points, 0, dim)
             fill_block(1, mate)
             fill_block(2, across)
-            near_second(wide.at[rounds], stage, leaf)
-            tree_finish(moved, 0, packed)
-            spread_transfers()
-            grp_copy(mine, theirs, 0).wait_recv()
-        else:
-            near_second(wide.at[rounds], stage, leaf)
-        tree_finish(skel.at[rounds], stage, rank)
-        sums = jnp.dot(spread_t[...], skel[rounds], preferred_element_type=f32).astype(bf16)
-        coup_out[rounds] = jnp.dot(theirs[...], sums, preferred_element_type=f32).astype(bf16)
-        grp_copy(coup_out.at[rounds], coup_in.at[rounds], stage).start()
-        level_one = jnp.dot(chosen[...], skel[rounds], preferred_element_type=f32)
+            near_second(points, 0, dim)
+            near_finish(points, 0, dim)
+        acc[...] += near_dot(rounds, 1, 3)
+        tree_sides(rounds)
         if rounds == 0:
             fill_block(3, me - 2 + 4 * row)
             fill_block(4, me - 1 + 2 * core)
+        near_second(wide.at[rounds], stage, leaf)
+        tree_wait(rounds, last_waits)
+        level_one = jnp.dot(partners[...], skel[rounds], preferred_element_type=f32)
         near_finish(wide.at[rounds], stage, leaf)
-        acc[...] += jnp.dot(
-            blocks[:, leaf:], wide[rounds, leaf:, :], preferred_element_type=f32
-        )
-        grp_copy(coup_out.at[rounds], coup_in.at[rounds], stage).wait_recv()
-        down = jnp.dot(transfer_rows, coup_in[rounds], preferred_element_type=f32)
+        acc[...] += near_dot(rounds, 3, 5)
+        down_all(rounds).wait_recv()
+        coupled = c_in[rounds].reshape(outs, rank)
+        down = lax.dot_general(
+            transfer_rows, coupled, (((1,), (1,)), ((), ())), preferred_element_type=f32
+        )
         far_part = jnp.dot(
             basis_p[...], (level_one + down).astype(bf16), preferred_element_type=f32
         )
@@ -472,12 +630,12 @@
         contraction = rho_next
 
     near_drain(points, 0, dim)
-    tree_drain(moved, 0, packed)
-    grp_copy(mine, theirs, 0).wait_send()
+    tag_all().wait_send()
     for rounds in range(ITERS):
         near_drain(wide.at[rounds], rounds + 1, leaf)
-        tree_drain(skel.at[rounds], rounds + 1, rank)
-        grp_copy(coup_out.at[rounds], coup_in.at[rounds], rounds + 1).wait_send()
+        tree_drain(rounds)
+        up_all(rounds).wait_send()
+        down_all(rounds).wait_send()
 
 
 def fused_body(
@@ -499,41 +657,52 @@
     outs = right_side.shape[1]
     rank = transfer.shape[1]
     clusters = cluster_couplings.shape[0]
+    width = outs // n
     bf16, f32 = jnp.bfloat16, jnp.float32
     vmem = pl.BlockSpec(memory_space=pltpu.VMEM)
     smem = pl.BlockSpec(memory_space=pltpu.SMEM)
+    hbm = pl.BlockSpec(memory_space=pltpu.HBM)
     sem = pltpu.SemaphoreType.DMA
     stages = ITERS + 1
     out = jax.ShapeDtypeStruct((leaf, outs), f32)
     return pl.pallas_call(
         functools.partial(fused_kernel, n),
         out_shape=(out, out),
-        in_specs=[vmem, vmem, vmem, smem, smem, vmem, vmem, vmem, smem, smem, vmem, vmem],
+        in_specs=[hbm, hbm, hbm, hbm, hbm, hbm, hbm, hbm, smem, hbm, hbm, hbm],
         out_specs=(vmem, vmem),
         scratch_shapes=[
             pltpu.VMEM((5 * dim, leaf), f32),
             pltpu.VMEM((ITERS, 5 * leaf, outs), bf16),
             pltpu.VMEM((leaf, 5 * leaf), bf16),
             pltpu.VMEM((ITERS, n * rank, outs), bf16),
-            pltpu.VMEM((n * (rank + 16), rank), bf16),
-            pltpu.VMEM((clusters * rank, n * rank), bf16),
+            pltpu.VMEM((ITERS, n, width + 16, rank), bf16),
+            pltpu.VMEM((ITERS, n, width + 16, rank), bf16),
+            pltpu.VMEM((n, 16, rank), bf16),
+            pltpu.VMEM((width, clusters * rank), bf16),
+            pltpu.VMEM((clusters * rank, clusters * rank), bf16),
             pltpu.VMEM((rank, n * rank), bf16),
-            pltpu.VMEM((rank, clusters * rank), bf16),
-            pltpu.VMEM((rank, clusters * rank), bf16),
-            pltpu.VMEM((ITERS, rank, outs), bf16),
-            pltpu.VMEM((ITERS, rank, outs), bf16),
+            pltpu.VMEM((ITERS, n, width, rank), bf16),
+            pltpu.VMEM((ITERS, n, width, rank), bf16),
             pltpu.VMEM((leaf, rank), bf16),
             pltpu.VMEM((rank, leaf), bf16),
             pltpu.VMEM((leaf, outs), f32),
             pltpu.VMEM((leaf, outs), f32),
+            pltpu.VMEM(leaf_perm.shape, jnp.int32),
+            pltpu.VMEM(leaf_basis.shape, bf16),
+            pltpu.VMEM(transfer.shape, bf16),
+            pltpu.VMEM(couplings.shape, bf16),
+            pltpu.VMEM(cluster_couplings.shape, bf16),
+            pltpu.VMEM((1, 1), f32),
+            pltpu.SMEM(near_list.shape, jnp.int32),
+            pltpu.SMEM(far_leaves.shape, jnp.int32),
+            pltpu.SMEM(far_clusters.shape, jnp.int32),
+            sem((11,)),
             sem((stages, 5, PARTS)),
             sem((stages, 5, PARTS)),
-            sem((stages, n // 2)),
-            sem((stages, n // 2)),
-            sem((stages, n // 2)),
-            sem((stages, n // 2)),
-            sem((stages,)),
-            sem((stages,)),
+            sem((ITERS, 15)),
+            sem((ITERS, n)),
+            sem((2 * ITERS + 1,)),
+            sem((2 * ITERS + 1,)),
         ],
         compiler_params=pltpu.CompilerParams(
             collective_id=0, has_side_effects=True, vmem_limit_bytes=48 << 20

time: 74.8 us -> 53.6 us (0.72)
  the two profiles are of different devices: /device:TPU:4 before, /device:TPU:16 now
where the time goes in v1:
time: 53.6 us; the launch traced here: 53.2 us
  Pallas kernels  43.4 us (81%)
  local copies, waits for them, and re-layouts  7.78 us (15%)
  between operations  2.01 us (4%)
    pallas_call x1, Pallas kernels, fused_body(): pl.pallas_call(functools.partial(fused_kernel, n), out_shape=(out, out),...  43.4 us
    unnamed x22, local copies, waits for them, and re-layouts  7.78 us

profile of v1, /device:TPU:16, one launch (start us, length us, event | category | flops | bytes accessed | tf_op | source)
XLA Modules:
  0.0 53.2 jit_solution(6344648342660651470)
XLA Ops:
  1.3 0.0 copy-start.7
  1.3 0.0 copy-start.6
  2.0 0.0 copy-start.8
  2.0 0.0 copy-start.9
  2.0 0.0 copy-done.7
  2.0 0.0 copy-done.6
  2.0 0.6 %copy-done.8 = s32[1,4]{1,0:T(1,128)S(1)} copy-done((s32[1,4]{1,0:T(1,128)S(1)}, s32[1,4]{1,0:T(1,128)}, u32[]{:S(2)}) %copy-start.8) | copy-done | bytes 40
  2.6 0.0 copy-done.9
  2.6 0.0 copy-start
  2.6 1.0 %copy-done = f32[512,256]{1,0:T(8,128)S(1)} copy-done((f32[512,256]{1,0:T(8,128)S(1)}, f32[512,256]{1,0:T(8,128)}, u32[]{:S(2)}) %copy-start) | copy-done | bytes 524312
  3.7 0.0 copy-start.1
  3.7 1.0 %copy-done.1 = bf16[4,4,128,128]{3,2,1,0:T(8,128)(2,1)S(1)} copy-done((bf16[4,4,128,128]{3,2,1,0:T(8,128)(2,1)S(1)}, bf16[4,4,128,128]{3,2,1,0:T(8,128)(2,1)}, u32[]{:S(2)}) %copy-start.1) | copy-done | bytes 524312
  4.7 0.0 copy-start.2
  4.7 0.9 %copy-done.2 = f32[512,64]{0,1:T(8,128)S(1)} copy-done((f32[512,64]{0,1:T(8,128)S(1)}, f32[512,64]{0,1:T(8,128)}, u32[]{:S(2)}) %copy-start.2) | copy-done | bytes 131096
  5.6 0.0 copy-start.3
  5.6 0.9 %copy-done.3 = bf16[1,4,128,128]{3,2,1,0:T(8,128)(2,1)S(1)} copy-done((bf16[1,4,128,128]{3,2,1,0:T(8,128)(2,1)S(1)}, bf16[1,4,128,128]{3,2,1,0:T(8,128)(2,1)}, u32[]{:S(2)}) %copy-start.3) | copy-done | bytes 131096
  6.5 0.0 copy-start.4
  6.5 0.9 %copy-done.4 = bf16[512,128]{1,0:T(8,128)(2,1)S(1)} copy-done((bf16[512,128]{1,0:T(8,128)(2,1)S(1)}, bf16[512,128]{1,0:T(8,128)(2,1)}, u32[]{:S(2)}) %copy-start.4) | copy-done | bytes 131096
  7.4 0.0 copy-start.5
  7.4 0.8 %copy-done.5 = bf16[1,128,128]{2,1,0:T(8,128)(2,1)S(1)} copy-done((bf16[1,128,128]{2,1,0:T(8,128)(2,1)S(1)}, bf16[1,128,128]{2,1,0:T(8,128)(2,1)}, u32[]{:S(2)}) %copy-start.5) | copy-done | bytes 32792
  8.2 43.4 %fused_solve.1 = (f32[512,256]{1,0:T(8,128)S(1)}, f32[512,256]{1,0:T(8,128)S(1)}) custom-call(f32[64,512]{1,0:T(8,128)S(1)} %bitcast.3, f32[512,256]{1,0:T(8,128)S(1)} %copy-done, s32[1,512]{1,0:T(1,128)S(1)} %copy-done.6, s32[1,4]{1,0:T(1,128)S(1)} %copy-done.8, s32[1,4]{1,0:T(1,128)S(1)} %copy-done.9, bf16[1,4,128,128]{3,2,1,0:T(8,128)(2,1)S(1)} %copy-done.3, ...), custom_call_target="tpu_custom_call" | custom-call | tf_op jit(solution)/shard_map/fused_solve/pallas_call | solution.py:668
  51.6 0.8 %copy.18 = f32[512,256]{1,0:T(8,128)} copy(f32[512,256]{1,0:T(8,128)S(1)} %get-tuple-element.4) | data formatting | bytes 1048576
  52.4 0.8 %copy.19 = f32[512,256]{1,0:T(8,128)} copy(f32[512,256]{1,0:T(8,128)S(1)} %get-tuple-element.5) | data formatting | bytes 1048576
Async XLA Ops:
  1.3 0.7 %copy-start.7 = (s32[4,4]{1,0:T(4,128)S(1)}, s32[4,4]{1,0:T(4,128)}, u32[]{:S(2)}) copy-start(s32[4,4]{1,0:T(4,128)} %farclus_hbm.1) | copy-start | bytes 196
  1.3 0.7 %copy-start.6 = (s32[1,512]{1,0:T(1,128)S(1)}, s32[1,512]{1,0:T(1,128)}, u32[]{:S(2)}) copy-start(s32[1,512]{1,0:T(1,128)} %perm_hbm.1) | copy-start | bytes 6148
  2.0 0.7 %copy-start.8 = (s32[1,4]{1,0:T(1,128)S(1)}, s32[1,4]{1,0:T(1,128)}, u32[]{:S(2)}) copy-start(s32[1,4]{1,0:T(1,128)} %near_hbm.1) | copy-start | bytes 52
  2.0 0.7 %copy-start.9 = (s32[1,4]{1,0:T(1,128)S(1)}, s32[1,4]{1,0:T(1,128)}, u32[]{:S(2)}) copy-start(s32[1,4]{1,0:T(1,128)} %far_hbm.1) | copy-start | bytes 52
  2.6 1.0 %copy-start = (f32[512,256]{1,0:T(8,128)S(1)}, f32[512,256]{1,0:T(8,128)}, u32[]{:S(2)}) copy-start(f32[512,256]{1,0:T(8,128)} %right_hbm.1) | copy-start | bytes 1572868
  3.7 1.0 %copy-start.1 = (bf16[4,4,128,128]{3,2,1,0:T(8,128)(2,1)S(1)}, bf16[4,4,128,128]{3,2,1,0:T(8,128)(2,1)}, u32[]{:S(2)}) copy-start(bf16[4,4,128,128]{3,2,1,0:T(8,128)(2,1)} %cluscoup_hbm.1) | copy-start | bytes 1572868
  4.7 0.9 %copy-start.2 = (f32[512,64]{0,1:T(8,128)S(1)}, f32[512,64]{0,1:T(8,128)}, u32[]{:S(2)}) copy-start(f32[512,64]{0,1:T(8,128)} %param.12) | copy-start | bytes 393220
  5.6 0.9 %copy-start.3 = (bf16[1,4,128,128]{3,2,1,0:T(8,128)(2,1)S(1)}, bf16[1,4,128,128]{3,2,1,0:T(8,128)(2,1)}, u32[]{:S(2)}) copy-start(bf16[1,4,128,128]{3,2,1,0:T(8,128)(2,1)} %coup_hbm.1) | copy-start | bytes 393220
  6.5 0.9 %copy-start.4 = (bf16[512,128]{1,0:T(8,128)(2,1)S(1)}, bf16[512,128]{1,0:T(8,128)(2,1)}, u32[]{:S(2)}) copy-start(bf16[512,128]{1,0:T(8,128)(2,1)} %basis_hbm.1) | copy-start | bytes 393220
  7.4 0.8 %copy-start.5 = (bf16[1,128,128]{2,1,0:T(8,128)(2,1)S(1)}, bf16[1,128,128]{2,1,0:T(8,128)(2,1)}, u32[]{:S(2)}) copy-start(bf16[1,128,128]{2,1,0:T(8,128)(2,1)} %transfer_hbm.1) | copy-start | bytes 98308

commit v2 on v1

--- a/solution.py
+++ b/solution.py
@@ -8,8 +8,8 @@
 from jax.sharding import PartitionSpec as P
 
 MESH = pl.DeviceIdType.MESH
-PARTS = 2
-EARLY = 1
+PARTS = 4
+EARLY = 2
 
 REACH = 2
 FARREACH = 8
@@ -152,7 +152,7 @@
     coup_hbm,
     transfer_hbm,
     basis_hbm,
-    cluster_ref,
+    cluster_hbm,
     farclus_hbm,
     cluscoup_hbm,
     ridge_hbm,
@@ -180,6 +180,7 @@
     coup_ref,
     cluscoup_ref,
     ridge_ref,
+    cluster_ref,
     near_ref,
     far_ref,
     farclus_ref,
@@ -205,8 +206,18 @@
     dim = coords_hbm.shape[0]
     rank = transfer_hbm.shape[1]
     clusters = cluscoup_hbm.shape[0]
-    width = outs // n
+    planes = n // 4
+    plane = lax.div(me, 4)
+    slicers = n // 2
+    width = outs // slicers
     tag_rows = 16
+    slices = (row == 1) == (plane < planes // 2)
+    my_slice = plane * 2 + core
+
+    def slicer(j):
+        side = jnp.where(lax.div(j, 2) < planes // 2, 2, 0)
+        return lax.div(j, 2) * 4 + side + lax.rem(j, 2)
+
     has_z = ((row == 0) & (me >= 4)) | ((row == 1) & (me + 4 < n))
     sends_z = ((row == 0) & (me + 4 < n)) | ((row == 1) & (me >= 4))
     z_target = jnp.where(sends_z, me + 4 - 8 * row, me)
@@ -223,6 +234,7 @@
     loads = {}
     for name, source, target in (
         ("perm", perm_hbm, perm_ref),
+        ("cluster", cluster_hbm, cluster_ref),
         ("basis", basis_hbm, basis_ref),
         ("ridge", ridge_hbm, ridge_ref),
         ("right", right_hbm, res_ref),
@@ -326,24 +338,27 @@
             device_id_type=MESH,
         )
 
-    along = (1, -1, 2, -2)
-    own_sends = [(inside(me + 4 * dz), me, me + 4 * dz) for dz in along]
-    own_sends.append((core == row, me, across_mate))
-    lane_waits, lane_sends = [], []
-    for dz in along:
-        owner = me - 4 * dz
+    ahead, behind = me + 4 * heading, me - 4 * heading
+    own_sends = [
+        (inside(ahead), me, ahead),
+        (inside(behind), me, behind),
+        (inside(ahead + 4 * heading), me, ahead + 4 * heading),
+        (inside(behind - 4 * heading), me, behind - 4 * heading),
+        (core == row, me, across_mate),
+    ]
+    lanes = []
+    for hops in (1, -1, -2, 2):
+        owner = me - 4 * heading * hops
         here = inside(owner)
-        lane_waits.append((here, owner))
-        passes = here
-        if dz == 2:
-            passes = here & (core == 1)
-        if dz == -2:
-            passes = here & (core == 0)
-        full = (heading == dz) | (heading * -2 == dz)
-        part = (heading == -dz) & (core == 1 - row)
-        lane_sends.append(
-            [(passes, owner, mate), (here & (full | part), owner, jnp.where(part, across_mate, across))]
-        )
+        if hops == 1:
+            sends = [(here, mate), (here, across)]
+        elif hops == -1:
+            sends = [(here, mate), (here & (core != row), across_mate)]
+        elif hops == -2:
+            sends = [(here, across), (here & (core == row), mate)]
+        else:
+            sends = [(here & (core != row), mate)]
+        lanes.append((here, owner, [(when, owner, target) for when, target in sends]))
     side_waits = [
         (inside(across + 4 * heading), across + 4 * heading),
         (inside(across - 8 * heading), across - 8 * heading),
@@ -359,7 +374,13 @@
         (inside(across_mate + 4 * heading), across_mate + 4 * heading),
         (inside(across_mate - 8 * heading), across_mate - 8 * heading),
     ]
-    every_send = own_sends + [pair for pairs in lane_sends for pair in pairs] + side_sends
+    every_send = list(own_sends)
+    lane_first = []
+    for _, _, sends in lanes:
+        lane_first.append(len(every_send))
+        every_send += sends
+    side_first = len(every_send)
+    every_send += side_sends
 
     def tree_go(rounds, first, sends):
         for step, (when, owner, target) in enumerate(sends):
@@ -377,13 +398,14 @@
 
     def tree_lanes(rounds, chosen):
         for lane in chosen:
-            tree_wait(rounds, lane_waits[lane : lane + 1])
-            tree_go(rounds, len(own_sends) + 2 * lane, lane_sends[lane])
+            here, owner, sends = lanes[lane]
+            tree_wait(rounds, [(here, owner)])
+            tree_go(rounds, lane_first[lane], sends)
 
     def tree_sides(rounds):
         for side in range(2):
             tree_wait(rounds, side_waits[side : side + 1])
-            tree_go(rounds, len(every_send) - 2 + side, side_sends[side : side + 1])
+            tree_go(rounds, side_first + side, side_sends[side : side + 1])
 
     def tree_drain(rounds):
         for step, (when, owner, target) in enumerate(every_send):
@@ -406,27 +428,30 @@
         return width + tag_rows if rounds == 0 else width
 
     def up_start(rounds):
-        for step in range(n):
-            place = lax.rem(me + n // 2 + step, n)
+        for step in range(slicers):
+            j = lax.rem(my_slice + slicers // 2 + step, slicers)
             rows = pl.ds(0, up_rows(rounds))
             wide_copy(
-                up_out.at[rounds, place, rows],
+                up_out.at[rounds, j, rows],
                 up_in.at[rounds, me, rows],
                 rounds,
-                {"grp": other, "dev": place},
+                {"grp": other, "dev": slicer(j)},
             ).start()
 
-    def up_all(rounds):
-        whole = up_in.at[rounds, pl.ds(0, n), pl.ds(0, up_rows(rounds))]
+    def up_all(rounds, count):
+        whole = up_in.at[rounds, pl.ds(0, count), pl.ds(0, up_rows(rounds))]
         return wide_copy(whole, whole, rounds, {"grp": other})
 
     def tag_start():
-        for step in range(1, n):
-            place = lax.rem(me + step, n)
-            wide_copy(tag_in.at[me], tag_in.at[me], ITERS, {"dev": place}).start()
-
-    def tag_all():
-        whole = tag_in.at[pl.ds(0, n - 1)]
+        for step in range(slicers):
+            place = slicer(lax.rem(my_slice + step, slicers))
+
+            @pl.when(place != me)
+            def _():
+                wide_copy(tag_in.at[me], tag_in.at[me], ITERS, {"dev": place}).start()
+
+    def tag_all(count):
+        whole = tag_in.at[pl.ds(0, count)]
         return wide_copy(whole, whole, ITERS, {"dev": mate})
 
     def down_start(rounds):
@@ -434,20 +459,21 @@
             place = lax.rem(me + step, n)
             wide_copy(
                 c_out.at[rounds, place],
-                c_in.at[rounds, me],
+                c_in.at[rounds, my_slice],
                 ITERS + 1 + rounds,
                 {"dev": place},
             ).start()
 
-    def down_all(rounds):
-        whole = c_in.at[rounds, pl.ds(0, n - 1)]
+    def down_all(rounds, count):
+        whole = c_out.at[rounds, pl.ds(0, count)]
         return wide_copy(whole, whole, ITERS + 1 + rounds, {"dev": mate})
 
-    local_cluster = cluster_ref[0] - group * clusters
+    loads["cluster"].wait()
+    local_cluster = cluster_ref[0, 0] - group * clusters
     lane_rows = lax.broadcasted_iota(jnp.int32, (tag_rows, rank), 0)
     tags = jnp.where(lane_rows == local_cluster, 1.0, 0.0).astype(bf16)
     tag_in[me] = tags
-    for place in range(n):
+    for place in range(slicers):
         up_out[0, place, width:, :] = tags
 
     loads["perm"].wait()
@@ -480,7 +506,7 @@
         uplift = jnp.dot(
             skeleton.T.astype(bf16), transfer_rows, preferred_element_type=f32
         ).astype(bf16)
-        for place in range(n):
+        for place in range(slicers):
             up_out[rounds, place, 0:width, :] = uplift[place * width : (place + 1) * width, :]
 
     def send(rounds):
@@ -520,26 +546,28 @@
                     skel[0, place * rank : (place + 1) * rank, :] = jnp.zeros((rank, outs), bf16)
 
     def couple(rounds):
-        up_all(rounds).wait_recv()
-        totals = [jnp.zeros((width, rank), f32) for _ in range(clusters)]
-        for place in range(n):
-            part = up_in[rounds, place, 0:width, :].astype(f32)
-            tag = up_in[0, place, width:, :].astype(f32)
-            totals = [totals[c] + tag[c : c + 1, :] * part for c in range(clusters)]
-        for c in range(clusters):
-            sums_t[:, c * rank : (c + 1) * rank] = totals[c].astype(bf16)
-        coupled = jnp.dot(sums_t[...], pair_map[...], preferred_element_type=f32)
-        coupled = coupled.astype(bf16).astype(f32)
-        if rounds == 0:
-            tag_all().wait_recv()
-        for place in range(n):
-            tag = tag_in[place].astype(f32)
-            pick = jnp.zeros((width, rank), f32)
+        @pl.when(slices)
+        def _():
+            up_all(rounds, n).wait_recv()
+            totals = [jnp.zeros((width, rank), f32) for _ in range(clusters)]
+            for place in range(n):
+                part = up_in[rounds, place, 0:width, :].astype(f32)
+                tag = up_in[0, place, width:, :].astype(f32)
+                totals = [totals[c] + tag[c : c + 1, :] * part for c in range(clusters)]
             for c in range(clusters):
-                pick = pick + tag[c : c + 1, :] * coupled[:, c * rank : (c + 1) * rank]
-            c_out[rounds, place] = pick.astype(bf16)
-        c_in[rounds, me] = c_out[rounds, me]
-        down_start(rounds)
+                sums_t[:, c * rank : (c + 1) * rank] = totals[c].astype(bf16)
+            coupled = jnp.dot(sums_t[...], pair_map[...], preferred_element_type=f32)
+            coupled = coupled.astype(bf16).astype(f32)
+            if rounds == 0:
+                tag_all(n - 1).wait_recv()
+            for place in range(n):
+                tag = tag_in[place].astype(f32)
+                pick = jnp.zeros((width, rank), f32)
+                for c in range(clusters):
+                    pick = pick + tag[c : c + 1, :] * coupled[:, c * rank : (c + 1) * rank]
+                c_out[rounds, place] = pick.astype(bf16)
+            c_in[rounds, my_slice] = c_out[rounds, me]
+            down_start(rounds)
 
     loads["coords"].wait()
     left = points[pl.ds(0, dim), :].T
@@ -575,45 +603,63 @@
     near_start(points, 0, dim)
     near_start(wide.at[0], 1, leaf)
     tree_go(0, 0, own_sends)
-    every = range(PARTS)
+    parts = range(PARTS)
     for rounds in range(ITERS):
         stage = rounds + 1
+        field = wide.at[rounds]
         if rounds > 0:
             prepare(rounds)
             send(rounds)
+            near_first(field, stage, leaf)
+            acc[...] = ridge * direction[...] + near_dot(rounds, 0, 2)
+            near_relay(field, stage, leaf, parts[:EARLY])
+            tree_lanes(rounds, (0, 1))
+            couple(rounds)
+            near_relay(field, stage, leaf, parts[EARLY:])
+            tree_lanes(rounds, (2, 3))
         else:
             fill_block(0, None)
+            loads["near"].wait()
+            near_first(points, 0, dim)
+            fill_block(1, mate)
             loads["farclus"].wait()
             loads["cluscoup"].wait()
             map_clusters()
             loads["far"].wait()
             loads["coup"].wait()
             map_partners()
-            near_relay(points, 0, dim, every)
-        acc[...] = ridge * direction[...] + near_dot(rounds, 0, 1)
-        near_relay(wide.at[rounds], stage, leaf, every[:EARLY])
-        couple(rounds)
-        near_relay(wide.at[rounds], stage, leaf, every[EARLY:])
-        tree_lanes(rounds, range(4))
-        near_first(wide.at[rounds], stage, leaf)
-        if rounds == 0:
-            loads["near"].wait()
-            near_first(points, 0, dim)
-            fill_block(1, mate)
+            near_relay(points, 0, dim, parts[:1])
+            near_first(field, stage, leaf)
+            acc[...] = ridge * direction[...] + near_dot(rounds, 0, 2)
+            near_relay(points, 0, dim, parts[1:])
+            tree_lanes(rounds, (0, 1))
+            couple(rounds)
             fill_block(2, across)
+            near_relay(field, stage, leaf, parts[:EARLY])
+            tree_lanes(rounds, (2,))
             near_second(points, 0, dim)
+            near_relay(field, stage, leaf, parts[EARLY:])
+            fill_block(3, me - 2 + 4 * row)
             near_finish(points, 0, dim)
-        acc[...] += near_dot(rounds, 1, 3)
+            fill_block(4, me - 1 + 2 * core)
+            tree_lanes(rounds, (3,))
+        acc[...] += near_dot(rounds, 2, 3)
         tree_sides(rounds)
-        if rounds == 0:
-            fill_block(3, me - 2 + 4 * row)
-            fill_block(4, me - 1 + 2 * core)
-        near_second(wide.at[rounds], stage, leaf)
+        near_second(field, stage, leaf)
+        acc[...] += near_dot(rounds, 3, 4)
         tree_wait(rounds, last_waits)
         level_one = jnp.dot(partners[...], skel[rounds], preferred_element_type=f32)
-        near_finish(wide.at[rounds], stage, leaf)
-        acc[...] += near_dot(rounds, 3, 5)
-        down_all(rounds).wait_recv()
+        near_finish(field, stage, leaf)
+        acc[...] += near_dot(rounds, 4, 5)
+
+        @pl.when(slices)
+        def _():
+            down_all(rounds, slicers - 1).wait_recv()
+
+        @pl.when(jnp.logical_not(slices))
+        def _():
+            down_all(rounds, slicers).wait_recv()
+
         coupled = c_in[rounds].reshape(outs, rank)
         down = lax.dot_general(
             transfer_rows, coupled, (((1,), (1,)), ((), ())), preferred_element_type=f32
@@ -630,12 +676,21 @@
         contraction = rho_next
 
     near_drain(points, 0, dim)
-    tag_all().wait_send()
+
+    @pl.when(slices)
+    def _():
+        tag_all(slicers - 1).wait_send()
+        for rounds in range(ITERS):
+            down_all(rounds, n - 1).wait_send()
+
+    @pl.when(jnp.logical_not(slices))
+    def _():
+        tag_all(slicers).wait_send()
+
     for rounds in range(ITERS):
         near_drain(wide.at[rounds], rounds + 1, leaf)
         tree_drain(rounds)
-        up_all(rounds).wait_send()
-        down_all(rounds).wait_send()
+        up_all(rounds, slicers).wait_send()
 
 
 def fused_body(
@@ -657,32 +712,36 @@
     outs = right_side.shape[1]
     rank = transfer.shape[1]
     clusters = cluster_couplings.shape[0]
-    width = outs // n
+    slicers = n // 2
+    width = outs // slicers
     bf16, f32 = jnp.bfloat16, jnp.float32
     vmem = pl.BlockSpec(memory_space=pltpu.VMEM)
-    smem = pl.BlockSpec(memory_space=pltpu.SMEM)
     hbm = pl.BlockSpec(memory_space=pltpu.HBM)
     sem = pltpu.SemaphoreType.DMA
     stages = ITERS + 1
+
+    def stay(array):
+        return pltpu.with_memory_space_constraint(array, pltpu.HBM)
+
     out = jax.ShapeDtypeStruct((leaf, outs), f32)
     return pl.pallas_call(
         functools.partial(fused_kernel, n),
         out_shape=(out, out),
-        in_specs=[hbm, hbm, hbm, hbm, hbm, hbm, hbm, hbm, smem, hbm, hbm, hbm],
+        in_specs=[hbm] * 12,
         out_specs=(vmem, vmem),
         scratch_shapes=[
             pltpu.VMEM((5 * dim, leaf), f32),
             pltpu.VMEM((ITERS, 5 * leaf, outs), bf16),
             pltpu.VMEM((leaf, 5 * leaf), bf16),
             pltpu.VMEM((ITERS, n * rank, outs), bf16),
-            pltpu.VMEM((ITERS, n, width + 16, rank), bf16),
+            pltpu.VMEM((ITERS, slicers, width + 16, rank), bf16),
             pltpu.VMEM((ITERS, n, width + 16, rank), bf16),
             pltpu.VMEM((n, 16, rank), bf16),
             pltpu.VMEM((width, clusters * rank), bf16),
             pltpu.VMEM((clusters * rank, clusters * rank), bf16),
             pltpu.VMEM((rank, n * rank), bf16),
             pltpu.VMEM((ITERS, n, width, rank), bf16),
-            pltpu.VMEM((ITERS, n, width, rank), bf16),
+            pltpu.VMEM((ITERS, slicers, width, rank), bf16),
             pltpu.VMEM((leaf, rank), bf16),
             pltpu.VMEM((rank, leaf), bf16),
             pltpu.VMEM((leaf, outs), f32),
@@ -693,13 +752,14 @@
             pltpu.VMEM(couplings.shape, bf16),
             pltpu.VMEM(cluster_couplings.shape, bf16),
             pltpu.VMEM((1, 1), f32),
+            pltpu.SMEM((1, 1), jnp.int32),
             pltpu.SMEM(near_list.shape, jnp.int32),
             pltpu.SMEM(far_leaves.shape, jnp.int32),
             pltpu.SMEM(far_clusters.shape, jnp.int32),
-            sem((11,)),
+            sem((12,)),
             sem((stages, 5, PARTS)),
             sem((stages, 5, PARTS)),
-            sem((ITERS, 15)),
+            sem((ITERS, 14)),
             sem((ITERS, n)),
             sem((2 * ITERS + 1,)),
             sem((2 * ITERS + 1,)),
@@ -709,17 +769,17 @@
         ),
         name="fused_solve",
     )(
-        coords.T,
-        right_side,
-        leaf_perm,
-        near_list,
-        far_leaves,
-        couplings,
-        transfer,
-        leaf_basis,
-        cluster_of,
-        far_clusters,
-        cluster_couplings,
+        stay(coords.T),
+        stay(right_side),
+        stay(leaf_perm),
+        stay(near_list),
+        stay(far_leaves),
+        stay(couplings),
+        stay(transfer),
+        stay(leaf_basis),
+        cluster_of.reshape(1, 1),
+        stay(far_clusters),
+        stay(cluster_couplings),
         ridge_weight.reshape(1, 1),
     )
 

time: 53.6 us -> 45.1 us (0.84)
  the two profiles are of different devices: /device:TPU:16 before, /device:TPU:5 now
where the time goes in v2:
time: 45.1 us; the launch traced here: 44.9 us
  Pallas kernels  41.3 us (92%)
  between operations  1.93 us (4%)
  local copies, waits for them, and re-layouts  1.59 us (4%)
    pallas_call x1, Pallas kernels, fused_body(): pl.pallas_call(functools.partial(fused_kernel, n), out_shape=(out, out),...  41.3 us
    unnamed x2, local copies, waits for them, and re-layouts  1.59 us

profile of v2, /device:TPU:5, one launch (start us, length us, event | category | flops | bytes accessed | tf_op | source)
XLA Modules:
  0.0 44.9 jit_solution(14111013062185567177)
XLA Ops:
  1.9 41.3 %fused_solve.1 = (f32[512,256]{1,0:T(8,128)S(1)}, f32[512,256]{1,0:T(8,128)S(1)}) custom-call(f32[64,512]{1,0:T(8,128)} %bitcast.5, f32[512,256]{1,0:T(8,128)} %right_hbm.1, s32[1,512]{1,0:T(1,128)} %perm_hbm.1, s32[1,4]{1,0:T(1,128)} %near_hbm.1, s32[1,4]{1,0:T(1,128)} %far_hbm.1, bf16[1,4,128,128]{3,2,1,0:T(8,128)(2,1)} %coup_hbm.1, ...), custom_call_target="tpu_custom_call" | custom-call | tf_op jit(solution)/shard_map/fused_solve/pallas_call | solution.py:727
  43.3 0.8 %copy.18 = f32[512,256]{1,0:T(8,128)} copy(f32[512,256]{1,0:T(8,128)S(1)} %get-tuple-element.4) | data formatting | bytes 1048576
  44.1 0.8 %copy.19 = f32[512,256]{1,0:T(8,128)} copy(f32[512,256]{1,0:T(8,128)S(1)} %get-tuple-element.5) | data formatting | bytes 1048576

commit v3 on v2

--- a/solution.py
+++ b/solution.py
@@ -142,6 +142,19 @@
     return (solution, residual)
 
 
+def interval(ridge):
+    bottom_edge = ridge + spectrum_gap
+    top_edge = ridge + spectrum_top
+    centre = (top_edge + bottom_edge) / 2.0
+    spread = (top_edge - bottom_edge) / 2.0
+    return centre, spread, centre / spread
+
+
+def momentum(sigma_ratio, spread, contraction):
+    rho_next = 1.0 / (2.0 * sigma_ratio - contraction)
+    return rho_next, rho_next * contraction, 2.0 * rho_next / spread
+
+
 def fused_kernel(
     n,
     coords_hbm,
@@ -158,6 +171,8 @@
     ridge_hbm,
     sol_ref,
     res_ref,
+    acc,
+    gain_ref,
     points,
     wide,
     blocks,
@@ -165,6 +180,7 @@
     up_out,
     up_in,
     tag_in,
+    up_tags,
     sums_t,
     pair_map,
     partners,
@@ -172,7 +188,8 @@
     c_in,
     basis_p,
     basis_t,
-    acc,
+    left_parts,
+    left_col,
     direction,
     perm_ref,
     basis_ref,
@@ -210,7 +227,6 @@
     plane = lax.div(me, 4)
     slicers = n // 2
     width = outs // slicers
-    tag_rows = 16
     slices = (row == 1) == (plane < planes // 2)
     my_slice = plane * 2 + core
 
@@ -424,34 +440,33 @@
             device_id_type=MESH,
         )
 
-    def up_rows(rounds):
-        return width + tag_rows if rounds == 0 else width
-
     def up_start(rounds):
         for step in range(slicers):
             j = lax.rem(my_slice + slicers // 2 + step, slicers)
-            rows = pl.ds(0, up_rows(rounds))
             wide_copy(
-                up_out.at[rounds, j, rows],
-                up_in.at[rounds, me, rows],
+                up_out.at[rounds, j],
+                up_in.at[rounds, me],
                 rounds,
                 {"grp": other, "dev": slicer(j)},
             ).start()
 
     def up_all(rounds, count):
-        whole = up_in.at[rounds, pl.ds(0, count), pl.ds(0, up_rows(rounds))]
+        whole = up_in.at[rounds, pl.ds(0, count)]
         return wide_copy(whole, whole, rounds, {"grp": other})
 
     def tag_start():
         for step in range(slicers):
             place = slicer(lax.rem(my_slice + step, slicers))
+            wide_copy(
+                tag_in.at[0, me], tag_in.at[1, me], ITERS, {"grp": other, "dev": place}
+            ).start()
 
             @pl.when(place != me)
             def _():
-                wide_copy(tag_in.at[me], tag_in.at[me], ITERS, {"dev": place}).start()
+                wide_copy(tag_in.at[0, me], tag_in.at[0, me], ITERS, {"dev": place}).start()
 
     def tag_all(count):
-        whole = tag_in.at[pl.ds(0, count)]
+        whole = up_tags.at[pl.ds(0, count)]
         return wide_copy(whole, whole, ITERS, {"dev": mate})
 
     def down_start(rounds):
@@ -470,11 +485,7 @@
 
     loads["cluster"].wait()
     local_cluster = cluster_ref[0, 0] - group * clusters
-    lane_rows = lax.broadcasted_iota(jnp.int32, (tag_rows, rank), 0)
-    tags = jnp.where(lane_rows == local_cluster, 1.0, 0.0).astype(bf16)
-    tag_in[me] = tags
-    for place in range(slicers):
-        up_out[0, place, width:, :] = tags
+    tag_in[0, me] = jnp.full((1, rank), local_cluster).astype(f32)
 
     loads["perm"].wait()
     targets = lax.broadcasted_iota(jnp.int32, (leaf, leaf), 0)
@@ -485,11 +496,7 @@
     basis_t[...] = placed.T.astype(bf16)
     loads["ridge"].wait()
     ridge = ridge_ref[...]
-    bottom_edge = ridge + spectrum_gap
-    top_edge = ridge + spectrum_top
-    centre = (top_edge + bottom_edge) / 2.0
-    spread = (top_edge - bottom_edge) / 2.0
-    sigma_ratio = centre / spread
+    centre, spread, sigma_ratio = interval(ridge)
     contraction = 1.0 / sigma_ratio
     loads["right"].wait()
     start = res_ref[...] / centre
@@ -507,7 +514,7 @@
             skeleton.T.astype(bf16), transfer_rows, preferred_element_type=f32
         ).astype(bf16)
         for place in range(slicers):
-            up_out[rounds, place, 0:width, :] = uplift[place * width : (place + 1) * width, :]
+            up_out[rounds, place] = uplift[place * width : (place + 1) * width, :]
 
     def send(rounds):
         up_start(rounds)
@@ -549,44 +556,56 @@
         @pl.when(slices)
         def _():
             up_all(rounds, n).wait_recv()
+            if rounds == 0:
+                tag_all(2 * n - 1).wait_recv()
             totals = [jnp.zeros((width, rank), f32) for _ in range(clusters)]
             for place in range(n):
-                part = up_in[rounds, place, 0:width, :].astype(f32)
-                tag = up_in[0, place, width:, :].astype(f32)
-                totals = [totals[c] + tag[c : c + 1, :] * part for c in range(clusters)]
+                part = up_in[rounds, place].astype(f32)
+                for c in range(clusters):
+                    mask = jnp.where(tag_in[1, place] == c, 1.0, 0.0)
+                    totals[c] = totals[c] + mask * part
             for c in range(clusters):
                 sums_t[:, c * rank : (c + 1) * rank] = totals[c].astype(bf16)
             coupled = jnp.dot(sums_t[...], pair_map[...], preferred_element_type=f32)
-            coupled = coupled.astype(bf16).astype(f32)
-            if rounds == 0:
-                tag_all(n - 1).wait_recv()
             for place in range(n):
-                tag = tag_in[place].astype(f32)
                 pick = jnp.zeros((width, rank), f32)
                 for c in range(clusters):
-                    pick = pick + tag[c : c + 1, :] * coupled[:, c * rank : (c + 1) * rank]
+                    mask = jnp.where(tag_in[0, place] == c, 1.0, 0.0)
+                    pick = pick + mask * coupled[:, c * rank : (c + 1) * rank]
                 c_out[rounds, place] = pick.astype(bf16)
             c_in[rounds, my_slice] = c_out[rounds, me]
             down_start(rounds)
 
     loads["coords"].wait()
-    left = points[pl.ds(0, dim), :].T
-    left_sq = jnp.sum(left * left, axis=1, keepdims=True)
+    log2e = 1.4426950408889634
+
+    def split(x):
+        high = x.astype(bf16).astype(f32)
+        middle = (x - high).astype(bf16).astype(f32)
+        return high, middle, x - high - middle
+
+    own = points[pl.ds(0, dim), :]
+    high, middle, low = split(own * (2.0 * kernel_scale * log2e))
+    left_parts[...] = (
+        jnp.concatenate([high, high, middle, middle, high, low], axis=0).T.astype(bf16)
+    )
+    left_sq = jnp.sum(own * own, axis=0, keepdims=True) * (kernel_scale * log2e)
+    left_col[...] = jnp.broadcast_to(left_sq, (128, leaf)).T
 
     def fill_block(slot, source):
         right = points[pl.ds(slot * dim, dim), :]
-        right_sq = jnp.sum(right * right, axis=0, keepdims=True)
-        inner = jnp.dot(
-            left, right, precision=lax.Precision.HIGHEST, preferred_element_type=f32
-        )
-        block = jnp.exp(-kernel_scale * (left_sq + right_sq - 2.0 * inner))
+        lift = jnp.sum(right * right, axis=0, keepdims=True) * (kernel_scale * log2e)
         if source is not None:
             wanted = group * n + source
             hit = jnp.float32(0.0)
             for k in range(near_ref.shape[1]):
                 listed = (near_ref[0, k] == wanted) & (near_ref[0, k] >= 0)
                 hit = hit + listed.astype(f32)
-            block = hit * block
+            lift = lift + (1.0 - hit) * 1e4
+        high, middle, low = split(right)
+        right_parts = jnp.concatenate([high, middle, high, middle, low, high], axis=0)
+        inner = jnp.dot(left_parts[...], right_parts.astype(bf16), preferred_element_type=f32)
+        block = jnp.exp2(inner - (left_col[:, 0:1] + lift))
         blocks[:, slot * leaf : (slot + 1) * leaf] = block.astype(bf16)
 
     def near_dot(rounds, first, last):
@@ -644,6 +663,10 @@
             fill_block(4, me - 1 + 2 * core)
             tree_lanes(rounds, (3,))
         acc[...] += near_dot(rounds, 2, 3)
+        if rounds == ITERS - 1:
+            _, keep, gain = momentum(sigma_ratio, spread, contraction)
+            gain_ref[...] = jnp.broadcast_to(gain, (1, outs))
+            sol_ref[...] += keep * direction[...]
         tree_sides(rounds)
         near_second(field, stage, leaf)
         acc[...] += near_dot(rounds, 3, 4)
@@ -667,10 +690,13 @@
         far_part = jnp.dot(
             basis_p[...], (level_one + down).astype(bf16), preferred_element_type=f32
         )
+        if rounds == ITERS - 1:
+            acc[...] += far_part
+            break
         residual = res_ref[...] - (acc[...] + far_part)
         res_ref[...] = residual
-        rho_next = 1.0 / (2.0 * sigma_ratio - contraction)
-        moved_on = rho_next * contraction * direction[...] + 2.0 * rho_next / spread * residual
+        rho_next, keep, gain = momentum(sigma_ratio, spread, contraction)
+        moved_on = keep * direction[...] + gain * residual
         direction[...] = moved_on
         sol_ref[...] += moved_on
         contraction = rho_next
@@ -679,13 +705,13 @@
 
     @pl.when(slices)
     def _():
-        tag_all(slicers - 1).wait_send()
+        tag_all(2 * slicers - 1).wait_send()
         for rounds in range(ITERS):
             down_all(rounds, n - 1).wait_send()
 
     @pl.when(jnp.logical_not(slices))
     def _():
-        tag_all(slicers).wait_send()
+        tag_all(2 * slicers).wait_send()
 
     for rounds in range(ITERS):
         near_drain(wide.at[rounds], rounds + 1, leaf)
@@ -724,19 +750,20 @@
         return pltpu.with_memory_space_constraint(array, pltpu.HBM)
 
     out = jax.ShapeDtypeStruct((leaf, outs), f32)
-    return pl.pallas_call(
+    base, residual, applied, gain = pl.pallas_call(
         functools.partial(fused_kernel, n),
-        out_shape=(out, out),
+        out_shape=(out, out, out, jax.ShapeDtypeStruct((1, outs), f32)),
         in_specs=[hbm] * 12,
-        out_specs=(vmem, vmem),
+        out_specs=(vmem, vmem, vmem, vmem),
         scratch_shapes=[
             pltpu.VMEM((5 * dim, leaf), f32),
             pltpu.VMEM((ITERS, 5 * leaf, outs), bf16),
             pltpu.VMEM((leaf, 5 * leaf), bf16),
             pltpu.VMEM((ITERS, n * rank, outs), bf16),
-            pltpu.VMEM((ITERS, slicers, width + 16, rank), bf16),
-            pltpu.VMEM((ITERS, n, width + 16, rank), bf16),
-            pltpu.VMEM((n, 16, rank), bf16),
+            pltpu.VMEM((ITERS, slicers, width, rank), bf16),
+            pltpu.VMEM((ITERS, n, width, rank), bf16),
+            pltpu.VMEM((2, n, 1, rank), f32),
+            pltpu.VMEM((2 * n, 1, rank), f32),
             pltpu.VMEM((width, clusters * rank), bf16),
             pltpu.VMEM((clusters * rank, clusters * rank), bf16),
             pltpu.VMEM((rank, n * rank), bf16),
@@ -744,7 +771,8 @@
             pltpu.VMEM((ITERS, slicers, width, rank), bf16),
             pltpu.VMEM((leaf, rank), bf16),
             pltpu.VMEM((rank, leaf), bf16),
-            pltpu.VMEM((leaf, outs), f32),
+            pltpu.VMEM((leaf, 6 * dim), bf16),
+            pltpu.VMEM((leaf, 128), f32),
             pltpu.VMEM((leaf, outs), f32),
             pltpu.VMEM(leaf_perm.shape, jnp.int32),
             pltpu.VMEM(leaf_basis.shape, bf16),
@@ -782,6 +810,8 @@
         stay(cluster_couplings),
         ridge_weight.reshape(1, 1),
     )
+    residual = residual - applied
+    return base + gain * residual, residual
 
 
 def solution(mesh):

time: 45.1 us -> 43.4 us (0.962)
  local copies, waits for them, and re-layouts: 1.59 us -> 0 us
  Pallas kernels: 41.3 us -> 40.2 us
  other arithmetic: 0 us -> 1.07 us
    unnamed x2 -> x0, local copies, waits for them, and re-layouts: 1.59 us -> none
    pallas_call x1, Pallas kernels: 41.3 us -> 40.2 us  [fused_body(): pl.pallas_call(functools.partial(fused_kernel, n), out_shape=(out, out, o...]
    add x0 -> x1, other arithmetic: none -> 1.07 us  [fused_body(): return (base + gain * residual, residual)]
where the time goes in v3:
time: 43.4 us; the launch traced here: 43.2 us
  Pallas kernels  40.2 us (93%)
  between operations  1.93 us (4%)
  other arithmetic  1.07 us (2%)
    pallas_call x1, Pallas kernels, fused_body(): pl.pallas_call(functools.partial(fused_kernel, n), out_shape=(out, out, o...  40.2 us
    add x1, other arithmetic, fused_body(): return (base + gain * residual, residual)  1.07 us

profile of v3, /device:TPU:5, one launch (start us, length us, event | category | flops | bytes accessed | tf_op | source)
XLA Modules:
  0.0 43.2 jit_solution(13751640715433061695)
XLA Ops:
  1.9 40.2 %fused_solve.1 = (f32[512,256]{1,0:T(8,128)S(1)}, f32[512,256]{1,0:T(8,128)S(1)}, f32[512,256]{1,0:T(8,128)S(1)}, f32[1,256]{1,0:T(1,128)S(1)}) custom-call(f32[64,512]{1,0:T(8,128)} %bitcast.7, f32[512,256]{1,0:T(8,128)} %right_hbm.1, s32[1,512]{1,0:T(1,128)} %perm_hbm.1, s32[1,4]{1,0:T(1,128)} %near_hbm.1, s32[1,4]{1,0:T(1,128)} %far_hbm.1, ...), custom_call_target="tpu_custom_call" | custom-call | tf_op jit(solution)/shard_map/fused_solve/pallas_call | solution.py:753
  42.1 1.1 %multiply_add_fusion = (f32[512,256]{1,0:T(8,128)}, f32[512,256]{1,0:T(8,128)}) fusion(f32[512,256]{1,0:T(8,128)S(1)} %get-tuple-element.6, f32[256]{0:T(256)S(1)} %bitcast.6, f32[512,256]{1,0:T(8,128)S(1)} %get-tuple-element.8, f32[512,256]{1,0:T(8,128)S(1)} %get-tuple-element.9), kind=kLoop, calls=%fused_computation | loop fusion | flops 393216 | bytes 2622464 | tf_op jit(solution)/shard_map/add | solution.py:814

commit v4 on v3

--- a/solution.py
+++ b/solution.py
@@ -670,8 +670,6 @@
         tree_sides(rounds)
         near_second(field, stage, leaf)
         acc[...] += near_dot(rounds, 3, 4)
-        tree_wait(rounds, last_waits)
-        level_one = jnp.dot(partners[...], skel[rounds], preferred_element_type=f32)
         near_finish(field, stage, leaf)
         acc[...] += near_dot(rounds, 4, 5)
 
@@ -687,6 +685,8 @@
         down = lax.dot_general(
             transfer_rows, coupled, (((1,), (1,)), ((), ())), preferred_element_type=f32
         )
+        tree_wait(rounds, last_waits)
+        level_one = jnp.dot(partners[...], skel[rounds], preferred_element_type=f32)
         far_part = jnp.dot(
             basis_p[...], (level_one + down).astype(bf16), preferred_element_type=f32
         )

time: 43.4 us -> 42.9 us (0.988)
  Pallas kernels: 40.2 us -> 39.7 us
    pallas_call x1, Pallas kernels: 40.2 us -> 39.7 us  [fused_body(): pl.pallas_call(functools.partial(fused_kernel, n), out_shape=(out, out, o...]
where the time goes in v4:
time: 42.9 us; the launch traced here: 42.7 us
  Pallas kernels  39.7 us (93%)
  between operations  1.93 us (4%)
  other arithmetic  1.07 us (2%)
    pallas_call x1, Pallas kernels, fused_body(): pl.pallas_call(functools.partial(fused_kernel, n), out_shape=(out, out, o...  39.7 us
    add x1, other arithmetic, fused_body(): return (base + gain * residual, residual)  1.07 us

profile of v4, /device:TPU:5, one launch (start us, length us, event | category | flops | bytes accessed | tf_op | source)
XLA Modules:
  0.0 42.7 jit_solution(11966592088701587971)
XLA Ops:
  1.9 39.7 %fused_solve.1 = (f32[512,256]{1,0:T(8,128)S(1)}, f32[512,256]{1,0:T(8,128)S(1)}, f32[512,256]{1,0:T(8,128)S(1)}, f32[1,256]{1,0:T(1,128)S(1)}) custom-call(f32[64,512]{1,0:T(8,128)} %bitcast.7, f32[512,256]{1,0:T(8,128)} %right_hbm.1, s32[1,512]{1,0:T(1,128)} %perm_hbm.1, s32[1,4]{1,0:T(1,128)} %near_hbm.1, s32[1,4]{1,0:T(1,128)} %far_hbm.1, ...), custom_call_target="tpu_custom_call" | custom-call | tf_op jit(solution)/shard_map/fused_solve/pallas_call | solution.py:753
  41.6 1.1 %multiply_add_fusion = (f32[512,256]{1,0:T(8,128)}, f32[512,256]{1,0:T(8,128)}) fusion(f32[512,256]{1,0:T(8,128)S(1)} %get-tuple-element.6, f32[256]{0:T(256)S(1)} %bitcast.6, f32[512,256]{1,0:T(8,128)S(1)} %get-tuple-element.8, f32[512,256]{1,0:T(8,128)S(1)} %get-tuple-element.9), kind=kLoop, calls=%fused_computation | loop fusion | flops 393216 | bytes 2622464 | tf_op jit(solution)/shard_map/add | solution.py:814

commit v5 on v4

--- a/solution.py
+++ b/solution.py
@@ -10,6 +10,7 @@
 MESH = pl.DeviceIdType.MESH
 PARTS = 4
 EARLY = 2
+LATE_TREE = (0,)
 
 REACH = 2
 FARREACH = 8
@@ -670,8 +671,9 @@
         tree_sides(rounds)
         near_second(field, stage, leaf)
         acc[...] += near_dot(rounds, 3, 4)
-        near_finish(field, stage, leaf)
-        acc[...] += near_dot(rounds, 4, 5)
+        if rounds in LATE_TREE:
+            near_finish(field, stage, leaf)
+            acc[...] += near_dot(rounds, 4, 5)
 
         @pl.when(slices)
         def _():
@@ -690,10 +692,13 @@
         far_part = jnp.dot(
             basis_p[...], (level_one + down).astype(bf16), preferred_element_type=f32
         )
+        acc[...] += far_part
+        if rounds not in LATE_TREE:
+            near_finish(field, stage, leaf)
+            acc[...] += near_dot(rounds, 4, 5)
         if rounds == ITERS - 1:
-            acc[...] += far_part
             break
-        residual = res_ref[...] - (acc[...] + far_part)
+        residual = res_ref[...] - acc[...]
         res_ref[...] = residual
         rho_next, keep, gain = momentum(sigma_ratio, spread, contraction)
         moved_on = keep * direction[...] + gain * residual

time: 42.9 us -> 42.4 us (0.988)
  Pallas kernels: 39.7 us -> 39.2 us
    pallas_call x1, Pallas kernels: 39.7 us -> 39.2 us  [fused_body(): pl.pallas_call(functools.partial(fused_kernel, n), out_shape=(out, out, o...]
where the time goes in v5:
time: 42.4 us; the launch traced here: 42.2 us
  Pallas kernels  39.2 us (92%)
  between operations  1.93 us (5%)
  other arithmetic  1.07 us (3%)
    pallas_call x1, Pallas kernels, fused_body(): pl.pallas_call(functools.partial(fused_kernel, n), out_shape=(out, out, o...  39.2 us
    add x1, other arithmetic, fused_body(): return (base + gain * residual, residual)  1.07 us

profile of v5, /device:TPU:5, one launch (start us, length us, event | category | flops | bytes accessed | tf_op | source)
XLA Modules:
  0.0 42.2 jit_solution(12286712551442305806)
XLA Ops:
  1.9 39.2 %fused_solve.1 = (f32[512,256]{1,0:T(8,128)S(1)}, f32[512,256]{1,0:T(8,128)S(1)}, f32[512,256]{1,0:T(8,128)S(1)}, f32[1,256]{1,0:T(1,128)S(1)}) custom-call(f32[64,512]{1,0:T(8,128)} %bitcast.7, f32[512,256]{1,0:T(8,128)} %right_hbm.1, s32[1,512]{1,0:T(1,128)} %perm_hbm.1, s32[1,4]{1,0:T(1,128)} %near_hbm.1, s32[1,4]{1,0:T(1,128)} %far_hbm.1, ...), custom_call_target="tpu_custom_call" | custom-call | tf_op jit(solution)/shard_map/fused_solve/pallas_call | solution.py:758
  41.1 1.1 %multiply_add_fusion = (f32[512,256]{1,0:T(8,128)}, f32[512,256]{1,0:T(8,128)}) fusion(f32[512,256]{1,0:T(8,128)S(1)} %get-tuple-element.6, f32[256]{0:T(256)S(1)} %bitcast.6, f32[512,256]{1,0:T(8,128)S(1)} %get-tuple-element.8, f32[512,256]{1,0:T(8,128)S(1)} %get-tuple-element.9), kind=kLoop, calls=%fused_computation | loop fusion | flops 393216 | bytes 2622464 | tf_op jit(solution)/shard_map/add | solution.py:819

commit v6 on v5

--- a/solution.py
+++ b/solution.py
@@ -632,11 +632,12 @@
             send(rounds)
             near_first(field, stage, leaf)
             acc[...] = ridge * direction[...] + near_dot(rounds, 0, 2)
+            tree_lanes(rounds, (0,))
             near_relay(field, stage, leaf, parts[:EARLY])
-            tree_lanes(rounds, (0, 1))
             couple(rounds)
+            tree_lanes(rounds, (2,))
             near_relay(field, stage, leaf, parts[EARLY:])
-            tree_lanes(rounds, (2, 3))
+            tree_lanes(rounds, (1, 3))
         else:
             fill_block(0, None)
             loads["near"].wait()

time: 42.4 us -> 42.4 us (level)
  no operation moved by 1% of the time
where the time goes in v6:
time: 42.4 us; the launch traced here: 42.2 us
  Pallas kernels  39.2 us (92%)
  between operations  1.93 us (5%)
  other arithmetic  1.07 us (3%)
    pallas_call x1, Pallas kernels, fused_body(): pl.pallas_call(functools.partial(fused_kernel, n), out_shape=(out, out, o...  39.2 us
    add x1, other arithmetic, fused_body(): return (base + gain * residual, residual)  1.07 us

profile of v6, /device:TPU:5, one launch (start us, length us, event | category | flops | bytes accessed | tf_op | source)
XLA Modules:
  0.0 42.2 jit_solution(11479792182840555809)
XLA Ops:
  1.9 39.2 %fused_solve.1 = (f32[512,256]{1,0:T(8,128)S(1)}, f32[512,256]{1,0:T(8,128)S(1)}, f32[512,256]{1,0:T(8,128)S(1)}, f32[1,256]{1,0:T(1,128)S(1)}) custom-call(f32[64,512]{1,0:T(8,128)} %bitcast.7, f32[512,256]{1,0:T(8,128)} %right_hbm.1, s32[1,512]{1,0:T(1,128)} %perm_hbm.1, s32[1,4]{1,0:T(1,128)} %near_hbm.1, s32[1,4]{1,0:T(1,128)} %far_hbm.1, ...), custom_call_target="tpu_custom_call" | custom-call | tf_op jit(solution)/shard_map/fused_solve/pallas_call | solution.py:759
  41.1 1.1 %multiply_add_fusion = (f32[512,256]{1,0:T(8,128)}, f32[512,256]{1,0:T(8,128)}) fusion(f32[512,256]{1,0:T(8,128)S(1)} %get-tuple-element.6, f32[256]{0:T(256)S(1)} %bitcast.6, f32[512,256]{1,0:T(8,128)S(1)} %get-tuple-element.8, f32[512,256]{1,0:T(8,128)S(1)} %get-tuple-element.9), kind=kLoop, calls=%fused_computation | loop fusion | flops 393216 | bytes 2622464 | tf_op jit(solution)/shard_map/add | solution.py:820
